TPU v7x, 512 devices: a whole 4x4x16 slice. The times are simulated.
512 devices in a mesh: ctx: 64 (over z_hi, x, y), head: 8 (over z_lo, core).
Axes of the slice: x: 4, y: 4, z: 16 (z_hi: 4, z_lo: 4; z = z_hi * 4 + z_lo), core: 2. Of those that a mesh axis runs over, the one named last changes fastest.
Arguments:
- queries: bfloat16 [16384, 6144], P(('ctx', 'head')), may hold values from -32 to 32
- keys: bfloat16 [16384, 6144], P(('ctx', 'head')), may hold values from -12 to 12
- values: bfloat16 [16384, 6144], P(('ctx', 'head')), may hold values from -6 to 6
- cache_keys: bfloat16 [32768, 6144], P('ctx', 'head'), may hold values from -6 to 6
- cache_values: bfloat16 [32768, 6144], P('ctx', 'head'), may hold values from -6 to 6
- pattern: int32 [128, 4], replicated, may hold values from 0 to 255, as said below
- reached: int32 [128], replicated, may hold values from 1 to 4, as said below
- gate: float32 [6144], replicated, may hold values from 0.5 to 2
Outputs:
- mixed: bfloat16 [16384, 6144], P(('ctx', 'head'))
Inputs may be any that keep to these rules, and one draw needn't show every extreme that they name: `pattern`: every entry of row g names a cached tile of ctx index g // 2 - 1, g // 2 or g // 2 + 1, where ctx index c holds cached tiles c * 4 to (c + 1) * 4 - 1. Only the first reached[g] entries of row g of pattern are used.
All inputs are finite; a program needn't handle non-finite values.
Results may differ from a plain program's by a relative error of at most 0.011.
Values may be sent and summed in bfloat16 or wider, within the bound.
No kernel may reach another device: no remote copies, remote signals or barrier semaphores. Data moves between devices by JAX's collectives and lax.ppermute only.
A program may use at most 64 MiB of HBM per device.

v0:
```python
import functools
import math

import jax
import jax.numpy as jnp
from jax import lax
from jax.experimental import pallas as pl
from jax.experimental.pallas import tpu as pltpu
from jax.sharding import PartitionSpec as P


HD = 128
TILE = 128
REACH = 4
NEGATIVE = -1e30
LIMIT = 16 << 20
PLANE = 16
SIDE = 4
Q_DETOUR = 96
O_DETOUR = 80
LOG2E = math.log2(math.e)
NT = (((1,), (1,)), ((), ()))


def vmem():
    return pl.BlockSpec(memory_space=pltpu.VMEM)


def smem():
    return pl.BlockSpec(memory_space=pltpu.SMEM)


def tile_bias(pattern_ref, reached_ref, tile, cached_id, tile_count):
    row = jnp.clip(tile, 0, tile_count - 1)
    used = reached_ref[row]
    times = jnp.int32(0)
    for slot in range(REACH):
        hit = jnp.logical_and(slot < used, pattern_ref[row, slot] == cached_id)
        times = times + jnp.where(hit, 1, 0)
    bias = jnp.where(times == 1, 0.0, NEGATIVE)
    bias = jnp.where(times == 2, 1.0, bias)
    bias = jnp.where(times == 3, math.log2(3.0), bias)
    return jnp.where(times == 4, 2.0, bias)


def fill_bias(bias_ref, pattern_ref, reached_ref, rel_tiles, own_tiles, cached_tiles):
    ctx = lax.axis_index("ctx")
    tile_count = pattern_ref.shape[0]
    for row, rel in enumerate(rel_tiles):
        for t in range(own_tiles):
            near = jnp.where(jnp.abs(rel - t) <= 2, 0.0, NEGATIVE)
            bias_ref[row, :, t * TILE : (t + 1) * TILE] = jnp.full((8, TILE), near, jnp.float32)
        for u in range(cached_tiles):
            bias = tile_bias(
                pattern_ref, reached_ref, ctx * own_tiles + rel, ctx * cached_tiles + u, tile_count
            )
            at = (own_tiles + u) * TILE
            bias_ref[row, :, at : at + TILE] = jnp.full((8, TILE), bias, jnp.float32)


def biased(scores, bias):
    scale = HD**-0.5 * LOG2E
    tiles = [scores[t * TILE : (t + 1) * TILE] * scale + row for t, row in enumerate(bias)]
    return jnp.concatenate(tiles, axis=0)


def attend(q, k, v, ck, cv, bias):
    near = lax.dot_general(q, k, NT, preferred_element_type=jnp.float32)
    far = lax.dot_general(q, ck, NT, preferred_element_type=jnp.float32)
    split = near.shape[1]
    near = biased(near, [row[:, :split] for row in bias])
    far = biased(far, [row[:, split:] for row in bias])
    peak = jnp.maximum(
        jnp.max(near, axis=1, keepdims=True), jnp.max(far, axis=1, keepdims=True)
    )
    near = jnp.exp2(near - peak)
    far = jnp.exp2(far - peak)
    total = jnp.sum(near, axis=1, keepdims=True) + jnp.sum(far, axis=1, keepdims=True)
    out = jnp.dot(near.astype(jnp.bfloat16), v, preferred_element_type=jnp.float32)
    out = out + jnp.dot(far.astype(jnp.bfloat16), cv, preferred_element_type=jnp.float32)
    return out / total, peak + jnp.log2(total)


def pieces(lse):
    lse = jnp.transpose(lse)[:16]
    high = lse.astype(jnp.bfloat16)
    rest = lse - high.astype(jnp.float32)
    middle = rest.astype(jnp.bfloat16)
    low = (rest - middle.astype(jnp.float32)).astype(jnp.bfloat16)
    return high, middle, low


def whole(rows):
    rows = rows.astype(jnp.float32)
    lse = rows[:, :TILE] + rows[:, TILE : 2 * TILE] + rows[:, 2 * TILE :]
    return jnp.transpose(jnp.concatenate([lse] * (HD // 16), axis=0))


def attend_all(load, rel_tiles, refs, put):
    pattern_ref, reached_ref, kv_ref, ck_ref, cv_ref, bias_ref = refs
    parts, _, part, width = kv_ref.shape
    rows = parts * part
    fill_bias(bias_ref, pattern_ref, reached_ref, rel_tiles, rows // TILE, ck_ref.shape[0] // TILE)
    bias = [bias_ref[t, 0:1, :] for t in range(rows // TILE)]
    lane = lax.broadcasted_iota(jnp.int32, (rows, HD), 1)
    stats = jnp.zeros((rows, HD), jnp.float32)
    for h in range(width // HD):
        cols = slice(h * HD, (h + 1) * HD)
        k = kv_ref[:, 0, :, cols].reshape(rows, HD)
        v = kv_ref[:, 1, :, cols].reshape(rows, HD)
        out, lse = attend(load(cols), k, v, ck_ref[:, cols], cv_ref[:, cols], bias)
        put(cols, out)
        stats = jnp.where(lane == h, lse, stats)
    put(None, stats)


def put_partial(o_ref, rows, cols, value):
    if cols is not None:
        o_ref[:rows, cols] = value.astype(jnp.bfloat16)
        return
    for t in range(rows // TILE):
        for i, piece in enumerate(pieces(value[t * TILE : (t + 1) * TILE])):
            o_ref[rows:, (3 * t + i) * TILE : (3 * t + i + 1) * TILE] = piece


def far_kernel(
    pattern_ref, reached_ref, below_ref, above_ref, kv_ref, ck_ref, cv_ref, to_below_ref, to_above_ref, *scratch
):
    own = kv_ref.shape[0] * kv_ref.shape[2] // TILE
    refs = (pattern_ref, reached_ref, kv_ref, ck_ref, cv_ref, *scratch)
    at = lax.rem(lax.axis_index("ctx"), PLANE)
    sides = ((below_ref, to_below_ref, at > 0, -own), (above_ref, to_above_ref, at < PLANE - 1, own))
    for q_ref, o_ref, inside, base in sides:

        @pl.when(inside)
        def _(q_ref=q_ref, o_ref=o_ref, base=base):
            def load(cols):
                return q_ref[:, cols]

            put = functools.partial(put_partial, o_ref, own * TILE)
            attend_all(load, [base + t for t in range(own)], refs, put)


def jump_kernel(*args):
    pattern_ref, reached_ref, *given = args[:5]
    kv_ref, _, _ = args[5:8]
    taken, o_ref, refs = args[8:11], args[11], (pattern_ref, reached_ref, *args[5:8], *args[12:])
    own = kv_ref.shape[0] * kv_ref.shape[2] // TILE
    at = lax.rem(lax.axis_index("ctx"), PLANE)

    @pl.when(jnp.logical_or(at == 0, at == PLANE - 1))
    def _():
        base = jnp.where(at == 0, -own, own)

        def load(cols):
            return joined(given, slice(0, own * TILE), cols)

        put = functools.partial(put_partial, o_ref, own * TILE)
        attend_all(load, [base + t for t in range(own)], refs, put)
        first = 0
        for ref in taken:
            ref[...] = o_ref[first : first + ref.shape[0]]
            first += ref.shape[0]


def joined(refs, rows, cols):
    found, first = [], 0
    for ref in refs:
        low, high = max(rows.start - first, 0), min(rows.stop - first, ref.shape[0])
        if low < high:
            found.append(ref[low:high, cols])
        first += ref.shape[0]
    return found[0] if len(found) == 1 else jnp.concatenate(found, axis=0)


def own_kernel(pattern_ref, reached_ref, q_ref, kv_ref, ck_ref, cv_ref, o_ref, stats_ref, bias_ref):
    def put(cols, value):
        if cols is None:
            stats_ref[...] = value
        else:
            o_ref[:, cols] = value

    own = kv_ref.shape[0] * kv_ref.shape[2] // TILE
    refs = (pattern_ref, reached_ref, kv_ref, ck_ref, cv_ref, bias_ref)
    attend_all(lambda cols: q_ref[:, cols], list(range(own)), refs, put)


def mix_kernel(count, o_ref, stats_ref, low_ref, high_ref, part0_ref, part1_ref, part2_ref, gate_ref, out_ref):
    parts = (part0_ref, part1_ref, part2_ref)
    ctx = lax.axis_index("ctx")
    at = lax.rem(ctx, PLANE)
    first, last = at == 0, at == PLANE - 1
    head = lax.axis_index("head")
    rows, width = o_ref.shape
    heads = width // HD
    for t in range(rows // TILE):
        here = slice(t * TILE, (t + 1) * TILE)
        stat = slice(rows, rows + 16), slice(3 * t * TILE, 3 * (t + 1) * TILE)
        jumped = joined(parts, *stat)
        low = whole(jnp.where(first, jumped, low_ref[stat]))
        high = whole(jnp.where(last, jumped, high_ref[stat]))
        low = jnp.where(ctx > 0, low, NEGATIVE)
        high = jnp.where(ctx < count - 1, high, NEGATIVE)
        mine = stats_ref[here, :]
        peak = jnp.maximum(jnp.maximum(mine, low), high)
        mine, low, high = jnp.exp2(mine - peak), jnp.exp2(low - peak), jnp.exp2(high - peak)
        total = 1.0 / (mine + low + high)
        mine, low, high = mine * total, low * total, high * total
        for h in range(heads):
            cols = slice(h * HD, (h + 1) * HD)
            jumped = joined(parts, here, cols)
            gate = gate_ref[pl.ds(head * heads + h, 1), :]
            mixed = o_ref[here, cols] * mine[:, h : h + 1]
            mixed = mixed + jnp.where(first, jumped, low_ref[here, cols]).astype(jnp.float32) * low[:, h : h + 1]
            mixed = mixed + jnp.where(last, jumped, high_ref[here, cols]).astype(jnp.float32) * high[:, h : h + 1]
            out_ref[here, cols] = (mixed * gate).astype(jnp.bfloat16)


def split_kernel(x_ref, out_ref, sems):
    count, _, width = out_ref.shape
    copies = [
        pltpu.make_async_copy(x_ref.at[:, i * width : (i + 1) * width], out_ref.at[i], sems.at[i]) for i in range(count)
    ]
    for copy in copies:
        copy.start()
    for copy in copies:
        copy.wait()


def attention_cost(tiles, rows, cached, width):
    pairs = tiles * TILE * (rows + cached)
    return pl.CostEstimate(
        flops=4 * pairs * width, bytes_accessed=4 * (rows + cached) * width, transcendentals=pairs * (width // HD)
    )


def local(queries, keys, values, cache_keys, cache_values, pattern, reached, gate):
    split = lax.axis_size("head")
    count = lax.axis_size("ctx")
    part, full = queries.shape
    width = full // split
    rows = part * split
    cached = cache_keys.shape[0]
    own = rows // TILE
    jumps = [(first - 1, first) for first in range(PLANE, count, PLANE)]
    corners = (PLANE - SIDE, SIDE - 1)
    up = [(i, i + 1) for i in range(count - 1) if (i + 1) % PLANE]
    down = [(b, a) for a, b in up]
    straight = jumps + [(b, a) for a, b in jumps]
    out, onward = [], []
    for rising, falling in (corners, corners[::-1]):
        ways = [(a, a + 1 - PLANE + rising, b) for a, b in jumps] + [(b, b + falling, a) for a, b in jumps]
        out.append([way[:2] for way in ways])
        onward.append([way[1:] for way in ways])

    def jump(x):
        return [shift(x[0], straight)] + [shift(shift(x[1 + i], out[i]), onward[i]) for i in range(2)]

    def shift(x, pairs):
        return lax.ppermute(x, "ctx", pairs)

    def blocks(x):
        return jnp.transpose(x.reshape(part, split, width), (1, 0, 2))

    q = pl.pallas_call(
        split_kernel,
        out_shape=jax.ShapeDtypeStruct((split, part, width), jnp.bfloat16),
        in_specs=[pl.BlockSpec(memory_space=pltpu.HBM)],
        out_specs=vmem(),
        scratch_shapes=[pltpu.SemaphoreType.DMA((split,))],
        compiler_params=pltpu.CompilerParams(vmem_limit_bytes=60 << 20),
        name="split",
    )(queries)
    q = lax.all_to_all(q, "head", split_axis=0, concat_axis=0, tiled=True).reshape(rows, width)
    kv = jnp.stack([blocks(keys), blocks(values)], axis=1)
    q, kv = lax.optimization_barrier((q, kv))
    cuts = (rows - 2 * Q_DETOUR, rows - Q_DETOUR)
    jumped = jump([q[: cuts[0]], q[cuts[0] : cuts[1]], q[cuts[1] :]])
    from_below = shift(q, up)
    from_above = shift(q, down)
    kv = lax.all_to_all(kv, "head", split_axis=0, concat_axis=0, tiled=True)

    partial = rows + 16

    def shapes(*counts):
        return tuple(jax.ShapeDtypeStruct((n, width), jnp.bfloat16) for n in counts)

    bias = pltpu.VMEM((own, 8, rows + cached), jnp.float32)
    to_below, to_above = pl.pallas_call(
        far_kernel,
        out_shape=shapes(partial, partial),
        in_specs=[smem(), smem()] + [vmem()] * 5,
        out_specs=(vmem(),) * 2,
        scratch_shapes=[bias],
        cost_estimate=attention_cost(2 * own, rows, cached, width),
        compiler_params=pltpu.CompilerParams(vmem_limit_bytes=LIMIT),
        name="far",
    )(pattern, reached, from_below, from_above, kv, cache_keys, cache_values)
    got_high = shift(to_below, down)
    got_low = shift(to_above, up)
    jumped = pl.pallas_call(
        jump_kernel,
        out_shape=shapes(partial - 2 * O_DETOUR, O_DETOUR, O_DETOUR),
        in_specs=[smem(), smem()] + [vmem()] * 6,
        out_specs=(vmem(),) * 3,
        scratch_shapes=[pltpu.VMEM((partial, width), jnp.bfloat16), bias],
        cost_estimate=attention_cost(own, rows, cached, width),
        compiler_params=pltpu.CompilerParams(vmem_limit_bytes=LIMIT),
        name="jump",
    )(pattern, reached, *jumped, kv, cache_keys, cache_values)
    jumped = jump(jumped)
    mine, stats = pl.pallas_call(
        own_kernel,
        out_shape=(
            jax.ShapeDtypeStruct((rows, width), jnp.float32),
            jax.ShapeDtypeStruct((rows, HD), jnp.float32),
        ),
        in_specs=[smem(), smem()] + [vmem()] * 4,
        out_specs=(vmem(), vmem()),
        scratch_shapes=[bias],
        cost_estimate=attention_cost(own, rows, cached, width),
        compiler_params=pltpu.CompilerParams(vmem_limit_bytes=LIMIT),
        name="own",
    )(pattern, reached, q, kv, cache_keys, cache_values)
    out = pl.pallas_call(
        functools.partial(mix_kernel, count),
        out_shape=jax.ShapeDtypeStruct((rows, width), jnp.bfloat16),
        in_specs=[vmem()] * 8,
        out_specs=vmem(),
        compiler_params=pltpu.CompilerParams(vmem_limit_bytes=LIMIT),
        name="mix",
    )(mine, stats, got_low, got_high, *jumped, gate.reshape(full // HD, HD))
    out = lax.all_to_all(out.reshape(split, part, width), "head", split_axis=0, concat_axis=0, tiled=True)
    return jnp.transpose(out, (1, 0, 2)).reshape(part, full)


def solution(mesh):
    tokens = P(("ctx", "head"), None)
    cached = P("ctx", "head")
    return jax.shard_map(
        local,
        mesh=mesh,
        in_specs=(tokens, tokens, tokens, cached, cached, P(), P(), P()),
        out_specs=tokens,
        check_vma=False,
    )
```

profile of v0, /device:TPU:30, one launch (start us, length us, event | category | flops | bytes accessed | tf_op | source)
XLA Modules:
  0.0 128.6 jit_solution(10691608991462528318)
XLA Ops:
  0.0 1.8 %split.1 = bf16[8,32,768]{2,1,0:T(8,128)(2,1)} custom-call(bf16[32,6144]{1,0:T(8,128)(2,1)} %x_ref.1), custom_call_target="tpu_custom_call" | custom-call | tf_op jit(solution)/shard_map/split/pallas_call | solution.py:265
  1.8 0.0 copy-start.4
  1.8 0.0 copy-start.5
  1.8 6.0 %all-to-all-start = ((bf16[8,32,768]{2,1,0:T(8,128)(2,1)}), bf16[8,32,768]{2,1,0:T(8,128)(2,1)S(1)}, u32[]{:S(2)}, u32[]{:S(2)}) async-start(bf16[8,32,768]{2,1,0:T(8,128)(2,1)} %split.1), calls=%async_computation | async-start | bytes 786432 | tf_op jit(solution)/shard_map/all_to_all | solution.py:274
  7.9 0.0 copy-done.4
  7.9 0.0 copy-done.5
  7.9 0.1 bitcast_bitcast_fusion
  8.0 1.0 pad_maximum_fusion
  8.9 11.4 %all-to-all-done = bf16[8,32,768]{2,1,0:T(8,128)(2,1)S(1)} async-done(((bf16[8,32,768]{2,1,0:T(8,128)(2,1)}), bf16[8,32,768]{2,1,0:T(8,128)(2,1)S(1)}, u32[]{:S(2)}, u32[]{:S(2)}) %all-to-all-start) | async-done | bytes 393248 | tf_op jit(solution)/shard_map/all_to_all | solution.py:274
  20.4 0.0 copy-start
  20.4 0.0 copy-start.1
  20.4 3.7 %all-to-all-start.1 = ((bf16[8,2,32,768]{3,2,1,0:T(8,128)(2,1)}), bf16[8,2,32,768]{3,2,1,0:T(8,128)(2,1)S(1)}, u32[]{:S(2)}, u32[]{:S(2)}) async-start(bf16[8,2,32,768]{3,2,1,0:T(8,128)(2,1)} %pad_maximum_fusion), calls=%async_computation.1 | async-start | bytes 1572864 | tf_op jit(solution)/shard_map/all_to_all | solution.py:281
  24.1 1.3 %collective-permute-start = (bf16[256,768]{1,0:T(8,128)(2,1)S(1)}, bf16[256,768]{1,0:T(8,128)(2,1)S(1)}, u32[]{:S(2)}, u32[]{:S(2)}) collective-permute-start(bf16[256,768]{1,0:T(8,128)(2,1)S(1)} %bitcast.20), channel_id=1, source_target_pairs={{0,8},{8,16},{16,24},{24,32},{32,40},{40,48},{48,56},{56,64},{64,7... | collective-permute-start | bytes 1179656 | tf_op jit(solution)/shard_map/ppermute | solution.py:260
  25.4 5.3 %collective-permute-start.1 = (bf16[256,768]{1,0:T(8,128)(2,1)S(1)}, bf16[256,768]{1,0:T(8,128)(2,1)}, u32[]{:S(2)}, u32[]{:S(2)}) collective-permute-start(bf16[256,768]{1,0:T(8,128)(2,1)S(1)} %bitcast.21), channel_id=1, source_target_pairs={{8,0},{16,8},{24,16},{32,24},{40,32},{48,40},{56,48},{64,56},{72,6... | collective-permute-start | bytes 1179656 | tf_op jit(solution)/shard_map/ppermute | solution.py:260
  30.7 0.0 copy-start.6
  30.7 4.2 %collective-permute-start.5 = (bf16[96,768]{1,0:T(8,128)(2,1)S(1)}, bf16[96,768]{1,0:T(8,128)(2,1)}, u32[]{:S(2)}, u32[]{:S(2)}) collective-permute-start(bf16[96,768]{1,0:T(8,128)(2,1)S(1)} %get-tuple-element.24), channel_id=1, source_target_pairs={{120,96},{248,224},{376,352},{128,152},{256,280},{384,408},{121,97... | collective-permute-start | bytes 442376 | tf_op jit(solution)/shard_map/ppermute | solution.py:260
  34.9 0.0 copy-start.3
  34.9 2.1 %collective-permute-start.7 = (bf16[96,768]{1,0:T(8,128)(2,1)S(1)}, bf16[96,768]{1,0:T(8,128)(2,1)}, u32[]{:S(2)}, u32[]{:S(2)}) collective-permute-start(bf16[96,768]{1,0:T(8,128)(2,1)S(1)} %get-tuple-element.23), channel_id=1, source_target_pairs={{120,24},{248,152},{376,280},{128,224},{256,352},{384,480},{121,25... | collective-permute-start | bytes 442376 | tf_op jit(solution)/shard_map/ppermute | solution.py:260
  36.9 0.0 copy-done.6
  36.9 0.1 copy.15.pattern_ref.args_0_
  37.1 2.1 %collective-permute-done.5 = bf16[96,768]{1,0:T(8,128)(2,1)} collective-permute-done((bf16[96,768]{1,0:T(8,128)(2,1)S(1)}, bf16[96,768]{1,0:T(8,128)(2,1)}, u32[]{:S(2)}, u32[]{:S(2)}) %collective-permute-start.5) | collective-permute-done | bytes 147488 | tf_op jit(solution)/shard_map/ppermute | solution.py:260
  39.2 1.3 collective-permute-start.6
  40.5 0.0 collective-permute-done.7
  40.5 1.3 %collective-permute-start.8 = (bf16[96,768]{1,0:T(8,128)(2,1)}, bf16[96,768]{1,0:T(8,128)(2,1)S(1)}, u32[]{:S(2)}, u32[]{:S(2)}) collective-permute-start(bf16[96,768]{1,0:T(8,128)(2,1)} %collective-permute-done.7), channel_id=1, source_target_pairs={{24,128},{152,256},{280,384},{224,120},{352,248},{480,376},{25,129... | collective-permute-start | bytes 442376 | tf_op jit(solution)/shard_map/ppermute | solution.py:260
  41.8 0.0 collective-permute-done.below_ref
  41.8 0.0 collective-permute-done.1.above_ref
  41.8 3.1 %all-to-all-done.1.kv_ref.args_5_ = bf16[8,2,32,768]{3,2,1,0:T(8,128)(2,1)S(1)} async-done(((bf16[8,2,32,768]{3,2,1,0:T(8,128)(2,1)}), bf16[8,2,32,768]{3,2,1,0:T(8,128)(2,1)S(1)}, u32[]{:S(2)}, u32[]{:S(2)}) %all-to-all-start.1) | async-done | bytes 786464 | tf_op jit(solution)/shard_map/all_to_all | solution.py:281
  44.9 0.0 copy-done
  44.9 0.0 copy-done.1
  44.9 0.0 copy-done.3
  44.9 4.2 %far.1 = (bf16[272,768]{1,0:T(8,128)(2,1)S(1)}, bf16[272,768]{1,0:T(8,128)(2,1)S(1)}) custom-call(s32[128,4]{1,0:T(8,128)S(1)} %copy.15.pattern_ref.args_0_, s32[128]{0:T(128)S(1)} %copy-done.3, bf16[256,768]{1,0:T(8,128)(2,1)S(1)} %collective-permute-done.below_ref, bf16[256,768]{1,0:T(8,128)(2,1)} %collective-permute-done.1.above_ref, ...), custom_call_target="tpu_custom_call" | custom-call | flops 1207959552 | bytes 2359296 | tf_op jit(solution)/shard_map/far/pallas_call | solution.py:289
  49.1 1.3 %collective-permute-start.2 = (bf16[272,768]{1,0:T(8,128)(2,1)S(1)}, bf16[272,768]{1,0:T(8,128)(2,1)S(1)}, u32[]{:S(2)}, u32[]{:S(2)}) collective-permute-start(bf16[272,768]{1,0:T(8,128)(2,1)S(1)} %get-tuple-element.18), channel_id=1, source_target_pairs={{0,8},{8,16},{16,24},{24,32},{32,40},{40,48},{48,56},{56,64},{64,7... | collective-permute-start | bytes 1253384 | tf_op jit(solution)/shard_map/ppermute | solution.py:260
  50.4 5.9 %collective-permute-start.3 = (bf16[272,768]{1,0:T(8,128)(2,1)S(1)}, bf16[272,768]{1,0:T(8,128)(2,1)S(1)}, u32[]{:S(2)}, u32[]{:S(2)}) collective-permute-start(bf16[272,768]{1,0:T(8,128)(2,1)S(1)} %get-tuple-element.19), channel_id=1, source_target_pairs={{8,0},{16,8},{24,16},{32,24},{40,32},{48,40},{56,48},{64,56},{72,6... | collective-permute-start | bytes 1253384 | tf_op jit(solution)/shard_map/ppermute | solution.py:260
  56.3 8.9 %collective-permute-start.4 = (bf16[64,768]{1,0:T(8,128)(2,1)S(1)}, bf16[64,768]{1,0:T(8,128)(2,1)S(1)}, u32[]{:S(2)}, u32[]{:S(2)}) collective-permute-start(bf16[64,768]{1,0:T(8,128)(2,1)S(1)} %slice.9), channel_id=1, source_target_pairs={{120,128},{248,256},{376,384},{128,120},{256,248},{384,376},{121,1... | collective-permute-start | bytes 294920 | tf_op jit(solution)/shard_map/ppermute | solution.py:260
  65.2 10.0 %collective-permute-done.4.args_2_ = bf16[64,768]{1,0:T(8,128)(2,1)S(1)} collective-permute-done((bf16[64,768]{1,0:T(8,128)(2,1)S(1)}, bf16[64,768]{1,0:T(8,128)(2,1)S(1)}, u32[]{:S(2)}, u32[]{:S(2)}) %collective-permute-start.4) | collective-permute-done | bytes 98336 | tf_op jit(solution)/shard_map/ppermute | solution.py:260
  75.3 0.0 collective-permute-done.6.args_3_
  75.3 0.0 collective-permute-done.8.args_4_
  75.3 4.3 %jump.1 = (bf16[112,768]{1,0:T(8,128)(2,1)S(1)}, bf16[80,768]{1,0:T(8,128)(2,1)S(1)}, bf16[80,768]{1,0:T(8,128)(2,1)S(1)}) custom-call(s32[128,4]{1,0:T(8,128)S(1)} %copy.15.pattern_ref.args_0_, s32[128]{0:T(128)S(1)} %copy-done.3, bf16[64,768]{1,0:T(8,128)(2,1)S(1)} %collective-permute-done.4.args_2_, bf16[96,768]{1,0:T(8,128)(2,1)S(1)} %collective-permute-done.6.args_3_, ...), custom_call_target="tpu_custom_call" | custom-call | flops 603979776 | bytes 2359296 | tf_op jit(solution)/shard_map/jump/pallas_call | solution.py:301
  79.5 1.3 %collective-permute-start.10 = (bf16[80,768]{1,0:T(8,128)(2,1)S(1)}, bf16[80,768]{1,0:T(8,128)(2,1)S(1)}, u32[]{:S(2)}, u32[]{:S(2)}) collective-permute-start(bf16[80,768]{1,0:T(8,128)(2,1)S(1)} %get-tuple-element.21), channel_id=1, source_target_pairs={{120,96},{248,224},{376,352},{128,152},{256,280},{384,408},{121,97... | collective-permute-start | bytes 368648 | tf_op jit(solution)/shard_map/ppermute | solution.py:260
  80.9 1.3 %collective-permute-start.12 = (bf16[80,768]{1,0:T(8,128)(2,1)S(1)}, bf16[80,768]{1,0:T(8,128)(2,1)S(1)}, u32[]{:S(2)}, u32[]{:S(2)}) collective-permute-start(bf16[80,768]{1,0:T(8,128)(2,1)S(1)} %get-tuple-element.22), channel_id=1, source_target_pairs={{120,24},{248,152},{376,280},{128,224},{256,352},{384,480},{121,25... | collective-permute-start | bytes 368648 | tf_op jit(solution)/shard_map/ppermute | solution.py:260
  82.2 0.0 copy-start.2
  82.2 4.8 %collective-permute-start.9 = (bf16[112,768]{1,0:T(8,128)(2,1)S(1)}, bf16[112,768]{1,0:T(8,128)(2,1)S(1)}, u32[]{:S(2)}, u32[]{:S(2)}) collective-permute-start(bf16[112,768]{1,0:T(8,128)(2,1)S(1)} %get-tuple-element.20), channel_id=1, source_target_pairs={{120,128},{248,256},{376,384},{128,120},{256,248},{384,376},{121,1... | collective-permute-start | bytes 516104 | tf_op jit(solution)/shard_map/ppermute | solution.py:260
  87.0 0.0 collective-permute-done.10
  87.0 1.3 %collective-permute-start.11 = (bf16[80,768]{1,0:T(8,128)(2,1)S(1)}, bf16[80,768]{1,0:T(8,128)(2,1)S(1)}, u32[]{:S(2)}, u32[]{:S(2)}) collective-permute-start(bf16[80,768]{1,0:T(8,128)(2,1)S(1)} %collective-permute-done.10), channel_id=1, source_target_pairs={{96,128},{224,256},{352,384},{152,120},{280,248},{408,376},{97,129... | collective-permute-start | bytes 368648 | tf_op jit(solution)/shard_map/ppermute | solution.py:260
  88.3 0.0 collective-permute-done.12
  88.3 1.5 %collective-permute-start.13 = (bf16[80,768]{1,0:T(8,128)(2,1)S(1)}, bf16[80,768]{1,0:T(8,128)(2,1)S(1)}, u32[]{:S(2)}, u32[]{:S(2)}) collective-permute-start(bf16[80,768]{1,0:T(8,128)(2,1)S(1)} %collective-permute-done.12), channel_id=1, source_target_pairs={{24,128},{152,256},{280,384},{224,120},{352,248},{480,376},{25,129... | collective-permute-start | bytes 368648 | tf_op jit(solution)/shard_map/ppermute | solution.py:260
  89.8 4.1 %own.1 = (f32[256,768]{1,0:T(8,128)S(1)}, f32[256,128]{1,0:T(8,128)S(1)}) custom-call(s32[128,4]{1,0:T(8,128)S(1)} %copy.15.pattern_ref.args_0_, s32[128]{0:T(128)S(1)} %copy-done.3, bf16[256,768]{1,0:T(8,128)(2,1)S(1)} %bitcast.24, bf16[8,2,32,768]{3,2,1,0:T(8,128)(2,1)S(1)} %all-to-all-done.1.kv_ref.args_5_, bf16[512,768]{1,0:T(8,128)(2,1)S(1)} %copy-done, ...), custom_call_target="tpu_custom_call" | custom-call | flops 603979776 | bytes 2359296 | tf_op jit(solution)/shard_map/own/pallas_call | solution.py:312
  93.9 12.6 %collective-permute-done.9.part0_ref = bf16[112,768]{1,0:T(8,128)(2,1)S(1)} collective-permute-done((bf16[112,768]{1,0:T(8,128)(2,1)S(1)}, bf16[112,768]{1,0:T(8,128)(2,1)S(1)}, u32[]{:S(2)}, u32[]{:S(2)}) %collective-permute-start.9) | collective-permute-done | bytes 172064 | tf_op jit(solution)/shard_map/ppermute | solution.py:260
  106.5 0.0 collective-permute-done.11.part1_ref
  106.5 4.0 %collective-permute-done.13.part2_ref = bf16[80,768]{1,0:T(8,128)(2,1)S(1)} collective-permute-done((bf16[80,768]{1,0:T(8,128)(2,1)S(1)}, bf16[80,768]{1,0:T(8,128)(2,1)S(1)}, u32[]{:S(2)}, u32[]{:S(2)}) %collective-permute-start.13) | collective-permute-done | bytes 122912 | tf_op jit(solution)/shard_map/ppermute | solution.py:260
  110.5 0.0 collective-permute-done.2.low_ref
  110.5 0.0 collective-permute-done.3.high_ref
  110.5 0.0 copy-done.2
  110.5 0.9 mix.1
  111.4 16.4 %all_to_all.15 = bf16[8,32,768]{2,1,0:T(8,128)(2,1)S(1)} all-to-all(bf16[8,32,768]{2,1,0:T(8,128)(2,1)S(1)} %bitcast.25), channel_id=1, replica_groups=mesh['ctx'=64,'head'=8] {'head'}, dimensions={0} | all-to-all | bytes 786432 | tf_op jit(solution)/shard_map/all_to_all | solution.py:333
  127.8 0.8 copy.21
  (2 shorter events, 0.0 us)
Async XLA Ops:
  1.8 6.1 %copy-start.4 = (bf16[32,6144]{1,0:T(8,128)(2,1)S(1)}, bf16[32,6144]{1,0:T(8,128)(2,1)}, u32[]{:S(2)}) copy-start(bf16[32,6144]{1,0:T(8,128)(2,1)} %param.10) | copy-start | bytes 1179652
  1.8 6.1 %copy-start.5 = (bf16[32,6144]{1,0:T(8,128)(2,1)S(1)}, bf16[32,6144]{1,0:T(8,128)(2,1)}, u32[]{:S(2)}) copy-start(bf16[32,6144]{1,0:T(8,128)(2,1)} %param.9) | copy-start | bytes 1179652
  1.8 18.6 %all-to-all-start = ((bf16[8,32,768]{2,1,0:T(8,128)(2,1)}), bf16[8,32,768]{2,1,0:T(8,128)(2,1)S(1)}, u32[]{:S(2)}, u32[]{:S(2)}) async-start(bf16[8,32,768]{2,1,0:T(8,128)(2,1)} %split.1), calls=%async_computation | async-start | bytes 786432 | tf_op jit(solution)/shard_map/all_to_all | solution.py:274
  20.4 24.6 %copy-start = (bf16[512,768]{1,0:T(8,128)(2,1)S(1)}, bf16[512,768]{1,0:T(8,128)(2,1)}, u32[]{:S(2)}) copy-start(bf16[512,768]{1,0:T(8,128)(2,1)} %args_6_.4) | copy-start | bytes 2359300
  20.4 24.6 %copy-start.1 = (bf16[512,768]{1,0:T(8,128)(2,1)S(1)}, bf16[512,768]{1,0:T(8,128)(2,1)}, u32[]{:S(2)}) copy-start(bf16[512,768]{1,0:T(8,128)(2,1)} %args_7_.4) | copy-start | bytes 2359300
  20.4 24.6 %all-to-all-start.1 = ((bf16[8,2,32,768]{3,2,1,0:T(8,128)(2,1)}), bf16[8,2,32,768]{3,2,1,0:T(8,128)(2,1)S(1)}, u32[]{:S(2)}, u32[]{:S(2)}) async-start(bf16[8,2,32,768]{3,2,1,0:T(8,128)(2,1)} %pad_maximum_fusion), calls=%async_computation.1 | async-start | bytes 1572864 | tf_op jit(solution)/shard_map/all_to_all | solution.py:281
  24.1 17.7 %collective-permute-start = (bf16[256,768]{1,0:T(8,128)(2,1)S(1)}, bf16[256,768]{1,0:T(8,128)(2,1)S(1)}, u32[]{:S(2)}, u32[]{:S(2)}) collective-permute-start(bf16[256,768]{1,0:T(8,128)(2,1)S(1)} %bitcast.20), channel_id=1, source_target_pairs={{0,8},{8,16},{16,24},{24,32},{32,40},{40,48},{48,56},{56,64},{64,7... | collective-permute-start | bytes 1179656 | tf_op jit(solution)/shard_map/ppermute | solution.py:260
  25.4 16.4 %collective-permute-start.1 = (bf16[256,768]{1,0:T(8,128)(2,1)S(1)}, bf16[256,768]{1,0:T(8,128)(2,1)}, u32[]{:S(2)}, u32[]{:S(2)}) collective-permute-start(bf16[256,768]{1,0:T(8,128)(2,1)S(1)} %bitcast.21), channel_id=1, source_target_pairs={{8,0},{16,8},{24,16},{32,24},{40,32},{48,40},{56,48},{64,56},{72,6... | collective-permute-start | bytes 1179656 | tf_op jit(solution)/shard_map/ppermute | solution.py:260
  30.7 6.2 %copy-start.6 = (s32[128,4]{0,1:T(4,128)S(1)}, s32[128,4]{0,1:T(4,128)}, u32[]{:S(2)}) copy-start(s32[128,4]{0,1:T(4,128)} %param.13) | copy-start | bytes 6148
  30.7 8.5 %collective-permute-start.5 = (bf16[96,768]{1,0:T(8,128)(2,1)S(1)}, bf16[96,768]{1,0:T(8,128)(2,1)}, u32[]{:S(2)}, u32[]{:S(2)}) collective-permute-start(bf16[96,768]{1,0:T(8,128)(2,1)S(1)} %get-tuple-element.24), channel_id=1, source_target_pairs={{120,96},{248,224},{376,352},{128,152},{256,280},{384,408},{121,97... | collective-permute-start | bytes 442376 | tf_op jit(solution)/shard_map/ppermute | solution.py:260
  34.9 10.1 %copy-start.3 = (s32[128]{0:T(128)S(1)}, s32[128]{0:T(128)}, u32[]{:S(2)}) copy-start(s32[128]{0:T(128)} %args_1_.4) | copy-start | bytes 1540
  34.9 5.6 %collective-permute-start.7 = (bf16[96,768]{1,0:T(8,128)(2,1)S(1)}, bf16[96,768]{1,0:T(8,128)(2,1)}, u32[]{:S(2)}, u32[]{:S(2)}) collective-permute-start(bf16[96,768]{1,0:T(8,128)(2,1)S(1)} %get-tuple-element.23), channel_id=1, source_target_pairs={{120,24},{248,152},{376,280},{128,224},{256,352},{384,480},{121,25... | collective-permute-start | bytes 442376 | tf_op jit(solution)/shard_map/ppermute | solution.py:260
  39.2 36.1 %collective-permute-start.6 = (bf16[96,768]{1,0:T(8,128)(2,1)}, bf16[96,768]{1,0:T(8,128)(2,1)S(1)}, u32[]{:S(2)}, u32[]{:S(2)}) collective-permute-start(bf16[96,768]{1,0:T(8,128)(2,1)} %collective-permute-done.5), channel_id=1, source_target_pairs={{96,128},{224,256},{352,384},{152,120},{280,248},{408,376},{97,129... | collective-permute-start | bytes 442376 | tf_op jit(solution)/shard_map/ppermute | solution.py:260
  40.5 34.8 %collective-permute-start.8 = (bf16[96,768]{1,0:T(8,128)(2,1)}, bf16[96,768]{1,0:T(8,128)(2,1)S(1)}, u32[]{:S(2)}, u32[]{:S(2)}) collective-permute-start(bf16[96,768]{1,0:T(8,128)(2,1)} %collective-permute-done.7), channel_id=1, source_target_pairs={{24,128},{152,256},{280,384},{224,120},{352,248},{480,376},{25,129... | collective-permute-start | bytes 442376 | tf_op jit(solution)/shard_map/ppermute | solution.py:260
  49.1 61.4 %collective-permute-start.2 = (bf16[272,768]{1,0:T(8,128)(2,1)S(1)}, bf16[272,768]{1,0:T(8,128)(2,1)S(1)}, u32[]{:S(2)}, u32[]{:S(2)}) collective-permute-start(bf16[272,768]{1,0:T(8,128)(2,1)S(1)} %get-tuple-element.18), channel_id=1, source_target_pairs={{0,8},{8,16},{16,24},{24,32},{32,40},{40,48},{48,56},{56,64},{64,7... | collective-permute-start | bytes 1253384 | tf_op jit(solution)/shard_map/ppermute | solution.py:260
  50.4 60.1 %collective-permute-start.3 = (bf16[272,768]{1,0:T(8,128)(2,1)S(1)}, bf16[272,768]{1,0:T(8,128)(2,1)S(1)}, u32[]{:S(2)}, u32[]{:S(2)}) collective-permute-start(bf16[272,768]{1,0:T(8,128)(2,1)S(1)} %get-tuple-element.19), channel_id=1, source_target_pairs={{8,0},{16,8},{24,16},{32,24},{40,32},{48,40},{56,48},{64,56},{72,6... | collective-permute-start | bytes 1253384 | tf_op jit(solution)/shard_map/ppermute | solution.py:260
  56.3 18.9 %collective-permute-start.4 = (bf16[64,768]{1,0:T(8,128)(2,1)S(1)}, bf16[64,768]{1,0:T(8,128)(2,1)S(1)}, u32[]{:S(2)}, u32[]{:S(2)}) collective-permute-start(bf16[64,768]{1,0:T(8,128)(2,1)S(1)} %slice.9), channel_id=1, source_target_pairs={{120,128},{248,256},{376,384},{128,120},{256,248},{384,376},{121,1... | collective-permute-start | bytes 294920 | tf_op jit(solution)/shard_map/ppermute | solution.py:260
  79.5 7.4 %collective-permute-start.10 = (bf16[80,768]{1,0:T(8,128)(2,1)S(1)}, bf16[80,768]{1,0:T(8,128)(2,1)S(1)}, u32[]{:S(2)}, u32[]{:S(2)}) collective-permute-start(bf16[80,768]{1,0:T(8,128)(2,1)S(1)} %get-tuple-element.21), channel_id=1, source_target_pairs={{120,96},{248,224},{376,352},{128,152},{256,280},{384,408},{121,97... | collective-permute-start | bytes 368648 | tf_op jit(solution)/shard_map/ppermute | solution.py:260
  80.9 7.4 %collective-permute-start.12 = (bf16[80,768]{1,0:T(8,128)(2,1)S(1)}, bf16[80,768]{1,0:T(8,128)(2,1)S(1)}, u32[]{:S(2)}, u32[]{:S(2)}) collective-permute-start(bf16[80,768]{1,0:T(8,128)(2,1)S(1)} %get-tuple-element.22), channel_id=1, source_target_pairs={{120,24},{248,152},{376,280},{128,224},{256,352},{384,480},{121,25... | collective-permute-start | bytes 368648 | tf_op jit(solution)/shard_map/ppermute | solution.py:260
  82.2 28.4 %copy-start.2 = (f32[6144]{0:T(1024)S(1)}, f32[6144]{0:T(1024)}, u32[]{:S(2)}) copy-start(f32[6144]{0:T(1024)} %param.15) | copy-start | bytes 73732
  82.2 24.3 %collective-permute-start.9 = (bf16[112,768]{1,0:T(8,128)(2,1)S(1)}, bf16[112,768]{1,0:T(8,128)(2,1)S(1)}, u32[]{:S(2)}, u32[]{:S(2)}) collective-permute-start(bf16[112,768]{1,0:T(8,128)(2,1)S(1)} %get-tuple-element.20), channel_id=1, source_target_pairs={{120,128},{248,256},{376,384},{128,120},{256,248},{384,376},{121,1... | collective-permute-start | bytes 516104 | tf_op jit(solution)/shard_map/ppermute | solution.py:260
  87.0 19.5 %collective-permute-start.11 = (bf16[80,768]{1,0:T(8,128)(2,1)S(1)}, bf16[80,768]{1,0:T(8,128)(2,1)S(1)}, u32[]{:S(2)}, u32[]{:S(2)}) collective-permute-start(bf16[80,768]{1,0:T(8,128)(2,1)S(1)} %collective-permute-done.10), channel_id=1, source_target_pairs={{96,128},{224,256},{352,384},{152,120},{280,248},{408,376},{97,129... | collective-permute-start | bytes 368648 | tf_op jit(solution)/shard_map/ppermute | solution.py:260
  88.3 22.2 %collective-permute-start.13 = (bf16[80,768]{1,0:T(8,128)(2,1)S(1)}, bf16[80,768]{1,0:T(8,128)(2,1)S(1)}, u32[]{:S(2)}, u32[]{:S(2)}) collective-permute-start(bf16[80,768]{1,0:T(8,128)(2,1)S(1)} %collective-permute-done.12), channel_id=1, source_target_pairs={{24,128},{152,256},{280,384},{224,120},{352,248},{480,376},{25,129... | collective-permute-start | bytes 368648 | tf_op jit(solution)/shard_map/ppermute | solution.py:260
where the time goes:
time: 129 us
  starting transfers between devices  51.3 us (40%)
  waiting for transfers between devices  43.4 us (34%)
  blocking collectives  16.4 us (13%)
  Pallas kernels  15.2 us (12%)
    ppermute x14, starting transfers between devices, shift(): return lax.ppermute(x, 'ctx', pairs)  41.6 us
    ppermute x14, waiting for transfers between devices, shift(): return lax.ppermute(x, 'ctx', pairs)  28.8 us
    all_to_all x1, blocking collectives, local(): lax.all_to_all(out.reshape(split, part, width), 'head', split_axis=0, con...  16.4 us
    all_to_all x1, waiting for transfers between devices, local(): lax.all_to_all(q, 'head', split_axis=0, concat_axis=0, tiled=True)  11.4 us
    all_to_all x1, starting transfers between devices, local(): lax.all_to_all(q, 'head', split_axis=0, concat_axis=0, tiled=True)  6.04 us
    pallas_call x1, Pallas kernels, local(): pl.pallas_call(jump_kernel, out_shape=shapes(partial - 2 * O_DETOUR, O_DE...  4.26 us
    pallas_call x1, Pallas kernels, local(): pl.pallas_call(far_kernel, out_shape=shapes(partial, partial), in_specs=[...  4.2 us
    pallas_call x1, Pallas kernels, local(): pl.pallas_call(own_kernel, out_shape=(jax.ShapeDtypeStruct((rows, width),...  4.14 us
  transfers between devices with their start and end apart: 16, of which 6 were waited for; matrix products, arithmetic and copies ran while one was open for 1% of the time, Pallas kernels for 10%

commit v1 on v0

--- a/solution.py
+++ b/solution.py
@@ -16,8 +16,7 @@
 LIMIT = 16 << 20
 PLANE = 16
 SIDE = 4
-Q_DETOUR = 96
-O_DETOUR = 80
+DETOUR = 96
 LOG2E = math.log2(math.e)
 NT = (((1,), (1,)), ((), ()))
 
@@ -216,17 +215,6 @@
             out_ref[here, cols] = (mixed * gate).astype(jnp.bfloat16)
 
 
-def split_kernel(x_ref, out_ref, sems):
-    count, _, width = out_ref.shape
-    copies = [
-        pltpu.make_async_copy(x_ref.at[:, i * width : (i + 1) * width], out_ref.at[i], sems.at[i]) for i in range(count)
-    ]
-    for copy in copies:
-        copy.start()
-    for copy in copies:
-        copy.wait()
-
-
 def attention_cost(tiles, rows, cached, width):
     pairs = tiles * TILE * (rows + cached)
     return pl.CostEstimate(
@@ -262,19 +250,10 @@
     def blocks(x):
         return jnp.transpose(x.reshape(part, split, width), (1, 0, 2))
 
-    q = pl.pallas_call(
-        split_kernel,
-        out_shape=jax.ShapeDtypeStruct((split, part, width), jnp.bfloat16),
-        in_specs=[pl.BlockSpec(memory_space=pltpu.HBM)],
-        out_specs=vmem(),
-        scratch_shapes=[pltpu.SemaphoreType.DMA((split,))],
-        compiler_params=pltpu.CompilerParams(vmem_limit_bytes=60 << 20),
-        name="split",
-    )(queries)
-    q = lax.all_to_all(q, "head", split_axis=0, concat_axis=0, tiled=True).reshape(rows, width)
+    q = lax.all_to_all(blocks(queries), "head", split_axis=0, concat_axis=0, tiled=True).reshape(rows, width)
     kv = jnp.stack([blocks(keys), blocks(values)], axis=1)
     q, kv = lax.optimization_barrier((q, kv))
-    cuts = (rows - 2 * Q_DETOUR, rows - Q_DETOUR)
+    cuts = (rows - 2 * DETOUR, rows - DETOUR)
     jumped = jump([q[: cuts[0]], q[cuts[0] : cuts[1]], q[cuts[1] :]])
     from_below = shift(q, up)
     from_above = shift(q, down)
@@ -300,7 +279,7 @@
     got_low = shift(to_above, up)
     jumped = pl.pallas_call(
         jump_kernel,
-        out_shape=shapes(partial - 2 * O_DETOUR, O_DETOUR, O_DETOUR),
+        out_shape=shapes(partial - 2 * DETOUR, DETOUR, DETOUR),
         in_specs=[smem(), smem()] + [vmem()] * 6,
         out_specs=(vmem(),) * 3,
         scratch_shapes=[pltpu.VMEM((partial, width), jnp.bfloat16), bias],

time: 129 us -> 125 us (0.969)
  the two profiles are of different devices: /device:TPU:30 before, /device:TPU:128 now
where the time goes in v1:
time: 125 us; the launch traced here: 124 us
  starting transfers between devices  50.5 us (40%)
  waiting for transfers between devices  30.8 us (25%)
  blocking collectives  25.7 us (21%)
  Pallas kernels  13.4 us (11%)
  local copies, waits for them, and re-layouts  2.79 us (2%)
    ppermute x14, starting transfers between devices, shift(): return lax.ppermute(x, 'ctx', pairs)  40.8 us
    all_to_all x1, blocking collectives, local(): lax.all_to_all(out.reshape(split, part, width), 'head', split_axis=0, con...  25.7 us
    ppermute x14, waiting for transfers between devices, shift(): return lax.ppermute(x, 'ctx', pairs)  19.3 us
    all_to_all x1, waiting for transfers between devices, local(): lax.all_to_all(blocks(queries), 'head', split_axis=0, concat_axis=0, tile...  11.4 us
    all_to_all x1, starting transfers between devices, local(): lax.all_to_all(blocks(queries), 'head', split_axis=0, concat_axis=0, tile...  6.03 us
    pallas_call x1, Pallas kernels, local(): pl.pallas_call(jump_kernel, out_shape=shapes(partial - 2 * DETOUR, DETOUR...  4.24 us
    pallas_call x1, Pallas kernels, local(): pl.pallas_call(far_kernel, out_shape=shapes(partial, partial), in_specs=[...  4.2 us
    pallas_call x1, Pallas kernels, local(): pl.pallas_call(own_kernel, out_shape=(jax.ShapeDtypeStruct((rows, width),...  4.13 us
  transfers between devices with their start and end apart: 16, of which 6 were waited for; matrix products, arithmetic and copies ran while one was open for 1% of the time, Pallas kernels for 10%

profile of v1, /device:TPU:128, one launch (start us, length us, event | category | flops | bytes accessed | tf_op | source)
XLA Modules:
  0.0 124.4 jit_solution(1001009896607739472)
XLA Ops:
  0.0 1.8 %copy.28 = bf16[4,8,8,768]{3,2,0,1:T(8,128)(2,1)} copy(bf16[4,8,8,768]{3,2,1,0:T(8,128)(2,1)} %bitcast.35) | data formatting | bytes 786432 | tf_op jit(solution)/shard_map/reshape | solution.py:251
  1.8 0.0 copy-start.4
  1.8 0.0 copy-start.5
  1.8 6.0 %all-to-all-start = ((bf16[8,32,768]{2,1,0:T(8,128)(2,1)}), bf16[8,32,768]{2,1,0:T(8,128)(2,1)S(1)}, u32[]{:S(2)}, u32[]{:S(2)}) async-start(bf16[8,32,768]{2,1,0:T(8,128)(2,1)} %bitcast.26), calls=%async_computation | async-start | bytes 786432 | tf_op jit(solution)/shard_map/all_to_all | solution.py:253
  7.8 0.0 copy-done.4
  7.8 0.0 copy-done.5
  7.8 0.1 bitcast_bitcast_fusion
  7.9 1.0 pad_maximum_fusion
  8.9 11.4 %all-to-all-done = bf16[8,32,768]{2,1,0:T(8,128)(2,1)S(1)} async-done(((bf16[8,32,768]{2,1,0:T(8,128)(2,1)}), bf16[8,32,768]{2,1,0:T(8,128)(2,1)S(1)}, u32[]{:S(2)}, u32[]{:S(2)}) %all-to-all-start) | async-done | bytes 393248 | tf_op jit(solution)/shard_map/all_to_all | solution.py:253
  20.3 0.0 copy-start.6
  20.3 0.0 copy-start.1
  20.3 3.7 %all-to-all-start.1 = ((bf16[8,2,32,768]{3,2,1,0:T(8,128)(2,1)}), bf16[8,2,32,768]{3,2,1,0:T(8,128)(2,1)S(1)}, u32[]{:S(2)}, u32[]{:S(2)}) async-start(bf16[8,2,32,768]{3,2,1,0:T(8,128)(2,1)} %pad_maximum_fusion), calls=%async_computation.1 | async-start | bytes 1572864 | tf_op jit(solution)/shard_map/all_to_all | solution.py:260
  24.0 0.0 copy-start
  24.0 4.4 %collective-permute-start = (bf16[256,768]{1,0:T(8,128)(2,1)S(1)}, bf16[256,768]{1,0:T(8,128)(2,1)}, u32[]{:S(2)}, u32[]{:S(2)}) collective-permute-start(bf16[256,768]{1,0:T(8,128)(2,1)S(1)} %bitcast.27), channel_id=1, source_target_pairs={{0,8},{8,16},{16,24},{24,32},{32,40},{40,48},{48,56},{56,64},{64,7... | collective-permute-start | bytes 1179656 | tf_op jit(solution)/shard_map/ppermute | solution.py:248
  28.4 1.3 %collective-permute-start.1 = (bf16[256,768]{1,0:T(8,128)(2,1)S(1)}, bf16[256,768]{1,0:T(8,128)(2,1)}, u32[]{:S(2)}, u32[]{:S(2)}) collective-permute-start(bf16[256,768]{1,0:T(8,128)(2,1)S(1)} %bitcast.28), channel_id=1, source_target_pairs={{8,0},{16,8},{24,16},{32,24},{40,32},{48,40},{56,48},{64,56},{72,6... | collective-permute-start | bytes 1179656 | tf_op jit(solution)/shard_map/ppermute | solution.py:248
  29.7 5.2 %collective-permute-start.5 = (bf16[96,768]{1,0:T(8,128)(2,1)S(1)}, bf16[96,768]{1,0:T(8,128)(2,1)S(1)}, u32[]{:S(2)}, u32[]{:S(2)}) collective-permute-start(bf16[96,768]{1,0:T(8,128)(2,1)S(1)} %get-tuple-element.24), channel_id=1, source_target_pairs={{120,96},{248,224},{376,352},{128,152},{256,280},{384,408},{121,97... | collective-permute-start | bytes 442376 | tf_op jit(solution)/shard_map/ppermute | solution.py:248
  35.0 3.8 %collective-permute-start.7 = (bf16[96,768]{1,0:T(8,128)(2,1)S(1)}, bf16[96,768]{1,0:T(8,128)(2,1)}, u32[]{:S(2)}, u32[]{:S(2)}) collective-permute-start(bf16[96,768]{1,0:T(8,128)(2,1)S(1)} %get-tuple-element.23), channel_id=1, source_target_pairs={{120,24},{248,152},{376,280},{128,224},{256,352},{384,480},{121,25... | collective-permute-start | bytes 442376 | tf_op jit(solution)/shard_map/ppermute | solution.py:248
  38.8 0.0 copy-done.6
  38.8 0.1 copy.17.pattern_ref.args_0_
  38.9 0.0 copy-start.3
  38.9 2.8 %collective-permute-start.4 = (bf16[64,768]{1,0:T(8,128)(2,1)S(1)}, bf16[64,768]{1,0:T(8,128)(2,1)S(1)}, u32[]{:S(2)}, u32[]{:S(2)}) collective-permute-start(bf16[64,768]{1,0:T(8,128)(2,1)S(1)} %slice.9), channel_id=1, source_target_pairs={{120,128},{248,256},{376,384},{128,120},{256,248},{384,376},{121,1... | collective-permute-start | bytes 294920 | tf_op jit(solution)/shard_map/ppermute | solution.py:248
  41.7 3.1 %collective-permute-done.5 = bf16[96,768]{1,0:T(8,128)(2,1)S(1)} collective-permute-done((bf16[96,768]{1,0:T(8,128)(2,1)S(1)}, bf16[96,768]{1,0:T(8,128)(2,1)S(1)}, u32[]{:S(2)}, u32[]{:S(2)}) %collective-permute-start.5) | collective-permute-done | bytes 147488 | tf_op jit(solution)/shard_map/ppermute | solution.py:248
  44.8 1.3 %collective-permute-start.6 = (bf16[96,768]{1,0:T(8,128)(2,1)S(1)}, bf16[96,768]{1,0:T(8,128)(2,1)S(1)}, u32[]{:S(2)}, u32[]{:S(2)}) collective-permute-start(bf16[96,768]{1,0:T(8,128)(2,1)S(1)} %collective-permute-done.5), channel_id=1, source_target_pairs={{96,128},{224,256},{352,384},{152,120},{280,248},{408,376},{97,129... | collective-permute-start | bytes 442376 | tf_op jit(solution)/shard_map/ppermute | solution.py:248
  46.1 0.0 collective-permute-done.7
  46.1 1.3 %collective-permute-start.8 = (bf16[96,768]{1,0:T(8,128)(2,1)}, bf16[96,768]{1,0:T(8,128)(2,1)S(1)}, u32[]{:S(2)}, u32[]{:S(2)}) collective-permute-start(bf16[96,768]{1,0:T(8,128)(2,1)} %collective-permute-done.7), channel_id=1, source_target_pairs={{24,128},{152,256},{280,384},{224,120},{352,248},{480,376},{25,129... | collective-permute-start | bytes 442376 | tf_op jit(solution)/shard_map/ppermute | solution.py:248
  47.4 0.0 collective-permute-done.below_ref
  47.4 0.0 collective-permute-done.1.above_ref
  47.5 0.0 all-to-all-done.1.kv_ref.args_5_
  47.5 0.0 copy-done.1
  47.5 0.0 copy-done
  47.5 0.0 copy-done.3
  47.5 4.2 %far.1 = (bf16[272,768]{1,0:T(8,128)(2,1)S(1)}, bf16[272,768]{1,0:T(8,128)(2,1)S(1)}) custom-call(s32[128,4]{1,0:T(8,128)S(1)} %copy.17.pattern_ref.args_0_, s32[128]{0:T(128)S(1)} %copy-done.3, bf16[256,768]{1,0:T(8,128)(2,1)} %collective-permute-done.below_ref, bf16[256,768]{1,0:T(8,128)(2,1)} %collective-permute-done.1.above_ref, ...), custom_call_target="tpu_custom_call" | custom-call | flops 1207959552 | bytes 2359296 | tf_op jit(solution)/shard_map/far/pallas_call | solution.py:268
  51.7 3.4 %collective-permute-start.2 = (bf16[272,768]{1,0:T(8,128)(2,1)S(1)}, bf16[272,768]{1,0:T(8,128)(2,1)S(1)}, u32[]{:S(2)}, u32[]{:S(2)}) collective-permute-start(bf16[272,768]{1,0:T(8,128)(2,1)S(1)} %get-tuple-element.18), channel_id=1, source_target_pairs={{0,8},{8,16},{16,24},{24,32},{32,40},{40,48},{48,56},{56,64},{64,7... | collective-permute-start | bytes 1253384 | tf_op jit(solution)/shard_map/ppermute | solution.py:248
  55.1 1.3 %collective-permute-start.3 = (bf16[272,768]{1,0:T(8,128)(2,1)S(1)}, bf16[272,768]{1,0:T(8,128)(2,1)S(1)}, u32[]{:S(2)}, u32[]{:S(2)}) collective-permute-start(bf16[272,768]{1,0:T(8,128)(2,1)S(1)} %get-tuple-element.19), channel_id=1, source_target_pairs={{8,0},{16,8},{24,16},{32,24},{40,32},{48,40},{56,48},{64,56},{72,6... | collective-permute-start | bytes 1253384 | tf_op jit(solution)/shard_map/ppermute | solution.py:248
  56.5 0.0 collective-permute-done.4.args_2_
  56.5 2.3 %collective-permute-done.6.args_3_ = bf16[96,768]{1,0:T(8,128)(2,1)S(1)} collective-permute-done((bf16[96,768]{1,0:T(8,128)(2,1)S(1)}, bf16[96,768]{1,0:T(8,128)(2,1)S(1)}, u32[]{:S(2)}, u32[]{:S(2)}) %collective-permute-start.6) | collective-permute-done | bytes 147488 | tf_op jit(solution)/shard_map/ppermute | solution.py:248
  58.8 1.5 %collective-permute-done.8.args_4_ = bf16[96,768]{1,0:T(8,128)(2,1)S(1)} collective-permute-done((bf16[96,768]{1,0:T(8,128)(2,1)}, bf16[96,768]{1,0:T(8,128)(2,1)S(1)}, u32[]{:S(2)}, u32[]{:S(2)}) %collective-permute-start.8) | collective-permute-done | bytes 147488 | tf_op jit(solution)/shard_map/ppermute | solution.py:248
  60.3 4.2 %jump.1 = (bf16[80,768]{1,0:T(8,128)(2,1)S(1)}, bf16[96,768]{1,0:T(8,128)(2,1)S(1)}, bf16[96,768]{1,0:T(8,128)(2,1)S(1)}) custom-call(s32[128,4]{1,0:T(8,128)S(1)} %copy.17.pattern_ref.args_0_, s32[128]{0:T(128)S(1)} %copy-done.3, bf16[64,768]{1,0:T(8,128)(2,1)S(1)} %collective-permute-done.4.args_2_, bf16[96,768]{1,0:T(8,128)(2,1)S(1)} %collective-permute-done.6.args_3_, ...), custom_call_target="tpu_custom_call" | custom-call | flops 603979776 | bytes 2359296 | tf_op jit(solution)/shard_map/jump/pallas_call | solution.py:280
  64.6 7.1 %collective-permute-start.10 = (bf16[96,768]{1,0:T(8,128)(2,1)S(1)}, bf16[96,768]{1,0:T(8,128)(2,1)S(1)}, u32[]{:S(2)}, u32[]{:S(2)}) collective-permute-start(bf16[96,768]{1,0:T(8,128)(2,1)S(1)} %get-tuple-element.21), channel_id=1, source_target_pairs={{120,96},{248,224},{376,352},{128,152},{256,280},{384,408},{121,97... | collective-permute-start | bytes 442376 | tf_op jit(solution)/shard_map/ppermute | solution.py:248
  71.7 3.4 %collective-permute-start.12 = (bf16[96,768]{1,0:T(8,128)(2,1)S(1)}, bf16[96,768]{1,0:T(8,128)(2,1)S(1)}, u32[]{:S(2)}, u32[]{:S(2)}) collective-permute-start(bf16[96,768]{1,0:T(8,128)(2,1)S(1)} %get-tuple-element.22), channel_id=1, source_target_pairs={{120,24},{248,152},{376,280},{128,224},{256,352},{384,480},{121,25... | collective-permute-start | bytes 442376 | tf_op jit(solution)/shard_map/ppermute | solution.py:248
  75.1 3.8 %collective-permute-done.10 = bf16[96,768]{1,0:T(8,128)(2,1)S(1)} collective-permute-done((bf16[96,768]{1,0:T(8,128)(2,1)S(1)}, bf16[96,768]{1,0:T(8,128)(2,1)S(1)}, u32[]{:S(2)}, u32[]{:S(2)}) %collective-permute-start.10) | collective-permute-done | bytes 147488 | tf_op jit(solution)/shard_map/ppermute | solution.py:248
  78.9 1.3 %collective-permute-start.11 = (bf16[96,768]{1,0:T(8,128)(2,1)S(1)}, bf16[96,768]{1,0:T(8,128)(2,1)S(1)}, u32[]{:S(2)}, u32[]{:S(2)}) collective-permute-start(bf16[96,768]{1,0:T(8,128)(2,1)S(1)} %collective-permute-done.10), channel_id=1, source_target_pairs={{96,128},{224,256},{352,384},{152,120},{280,248},{408,376},{97,129... | collective-permute-start | bytes 442376 | tf_op jit(solution)/shard_map/ppermute | solution.py:248
  80.2 0.0 collective-permute-done.12
  80.2 1.3 %collective-permute-start.13 = (bf16[96,768]{1,0:T(8,128)(2,1)S(1)}, bf16[96,768]{1,0:T(8,128)(2,1)S(1)}, u32[]{:S(2)}, u32[]{:S(2)}) collective-permute-start(bf16[96,768]{1,0:T(8,128)(2,1)S(1)} %collective-permute-done.12), channel_id=1, source_target_pairs={{24,128},{152,256},{280,384},{224,120},{352,248},{480,376},{25,129... | collective-permute-start | bytes 442376 | tf_op jit(solution)/shard_map/ppermute | solution.py:248
  81.5 0.0 copy-start.2
  81.5 2.9 %collective-permute-start.9 = (bf16[80,768]{1,0:T(8,128)(2,1)S(1)}, bf16[80,768]{1,0:T(8,128)(2,1)S(1)}, u32[]{:S(2)}, u32[]{:S(2)}) collective-permute-start(bf16[80,768]{1,0:T(8,128)(2,1)S(1)} %get-tuple-element.20), channel_id=1, source_target_pairs={{120,128},{248,256},{376,384},{128,120},{256,248},{384,376},{121,1... | collective-permute-start | bytes 368648 | tf_op jit(solution)/shard_map/ppermute | solution.py:248
  84.4 4.1 %own.1 = (f32[256,768]{1,0:T(8,128)S(1)}, f32[256,128]{1,0:T(8,128)S(1)}) custom-call(s32[128,4]{1,0:T(8,128)S(1)} %copy.17.pattern_ref.args_0_, s32[128]{0:T(128)S(1)} %copy-done.3, bf16[256,768]{1,0:T(8,128)(2,1)S(1)} %bitcast.31, bf16[8,2,32,768]{3,2,1,0:T(8,128)(2,1)S(1)} %all-to-all-done.1.kv_ref.args_5_, bf16[512,768]{1,0:T(8,128)(2,1)S(1)} %copy-done, ...), custom_call_target="tpu_custom_call" | custom-call | flops 603979776 | bytes 2359296 | tf_op jit(solution)/shard_map/own/pallas_call | solution.py:291
  88.6 8.5 %collective-permute-done.9.part0_ref = bf16[80,768]{1,0:T(8,128)(2,1)S(1)} collective-permute-done((bf16[80,768]{1,0:T(8,128)(2,1)S(1)}, bf16[80,768]{1,0:T(8,128)(2,1)S(1)}, u32[]{:S(2)}, u32[]{:S(2)}) %collective-permute-start.9) | collective-permute-done | bytes 122912 | tf_op jit(solution)/shard_map/ppermute | solution.py:248
  97.1 0.0 collective-permute-done.11.part1_ref
  97.1 0.0 collective-permute-done.13.part2_ref
  97.1 0.0 collective-permute-done.2.low_ref
  97.1 0.0 collective-permute-done.3.high_ref
  97.1 0.0 copy-done.2
  97.1 0.8 mix.1
  97.9 25.7 %all_to_all.15 = bf16[8,32,768]{2,1,0:T(8,128)(2,1)S(1)} all-to-all(bf16[8,32,768]{2,1,0:T(8,128)(2,1)S(1)} %bitcast.32), channel_id=1, replica_groups=mesh['ctx'=64,'head'=8] {'head'}, dimensions={0} | all-to-all | bytes 786432 | tf_op jit(solution)/shard_map/all_to_all | solution.py:312
  123.7 0.8 copy.24
  (2 shorter events, 0.0 us)
Async XLA Ops:
  1.8 6.0 %copy-start.4 = (bf16[32,6144]{1,0:T(8,128)(2,1)S(1)}, bf16[32,6144]{1,0:T(8,128)(2,1)}, u32[]{:S(2)}) copy-start(bf16[32,6144]{1,0:T(8,128)(2,1)} %param.10) | copy-start | bytes 1179652
  1.8 6.0 %copy-start.5 = (bf16[32,6144]{1,0:T(8,128)(2,1)S(1)}, bf16[32,6144]{1,0:T(8,128)(2,1)}, u32[]{:S(2)}) copy-start(bf16[32,6144]{1,0:T(8,128)(2,1)} %param.9) | copy-start | bytes 1179652
  1.8 18.6 %all-to-all-start = ((bf16[8,32,768]{2,1,0:T(8,128)(2,1)}), bf16[8,32,768]{2,1,0:T(8,128)(2,1)S(1)}, u32[]{:S(2)}, u32[]{:S(2)}) async-start(bf16[8,32,768]{2,1,0:T(8,128)(2,1)} %bitcast.26), calls=%async_computation | async-start | bytes 786432 | tf_op jit(solution)/shard_map/all_to_all | solution.py:253
  20.3 18.5 %copy-start.6 = (s32[128,4]{0,1:T(4,128)S(1)}, s32[128,4]{0,1:T(4,128)}, u32[]{:S(2)}) copy-start(s32[128,4]{0,1:T(4,128)} %param.13) | copy-start | bytes 6148
  20.3 27.1 %copy-start.1 = (bf16[512,768]{1,0:T(8,128)(2,1)S(1)}, bf16[512,768]{1,0:T(8,128)(2,1)}, u32[]{:S(2)}) copy-start(bf16[512,768]{1,0:T(8,128)(2,1)} %args_7_.4) | copy-start | bytes 2359300
  20.3 27.1 %all-to-all-start.1 = ((bf16[8,2,32,768]{3,2,1,0:T(8,128)(2,1)}), bf16[8,2,32,768]{3,2,1,0:T(8,128)(2,1)S(1)}, u32[]{:S(2)}, u32[]{:S(2)}) async-start(bf16[8,2,32,768]{3,2,1,0:T(8,128)(2,1)} %pad_maximum_fusion), calls=%async_computation.1 | async-start | bytes 1572864 | tf_op jit(solution)/shard_map/all_to_all | solution.py:260
  24.0 23.5 %copy-start = (bf16[512,768]{1,0:T(8,128)(2,1)S(1)}, bf16[512,768]{1,0:T(8,128)(2,1)}, u32[]{:S(2)}) copy-start(bf16[512,768]{1,0:T(8,128)(2,1)} %args_6_.4) | copy-start | bytes 2359300
  24.0 23.4 %collective-permute-start = (bf16[256,768]{1,0:T(8,128)(2,1)S(1)}, bf16[256,768]{1,0:T(8,128)(2,1)}, u32[]{:S(2)}, u32[]{:S(2)}) collective-permute-start(bf16[256,768]{1,0:T(8,128)(2,1)S(1)} %bitcast.27), channel_id=1, source_target_pairs={{0,8},{8,16},{16,24},{24,32},{32,40},{40,48},{48,56},{56,64},{64,7... | collective-permute-start | bytes 1179656 | tf_op jit(solution)/shard_map/ppermute | solution.py:248
  28.4 19.0 %collective-permute-start.1 = (bf16[256,768]{1,0:T(8,128)(2,1)S(1)}, bf16[256,768]{1,0:T(8,128)(2,1)}, u32[]{:S(2)}, u32[]{:S(2)}) collective-permute-start(bf16[256,768]{1,0:T(8,128)(2,1)S(1)} %bitcast.28), channel_id=1, source_target_pairs={{8,0},{16,8},{24,16},{32,24},{40,32},{48,40},{56,48},{64,56},{72,6... | collective-permute-start | bytes 1179656 | tf_op jit(solution)/shard_map/ppermute | solution.py:248
  29.7 15.1 %collective-permute-start.5 = (bf16[96,768]{1,0:T(8,128)(2,1)S(1)}, bf16[96,768]{1,0:T(8,128)(2,1)S(1)}, u32[]{:S(2)}, u32[]{:S(2)}) collective-permute-start(bf16[96,768]{1,0:T(8,128)(2,1)S(1)} %get-tuple-element.24), channel_id=1, source_target_pairs={{120,96},{248,224},{376,352},{128,152},{256,280},{384,408},{121,97... | collective-permute-start | bytes 442376 | tf_op jit(solution)/shard_map/ppermute | solution.py:248
  35.0 11.1 %collective-permute-start.7 = (bf16[96,768]{1,0:T(8,128)(2,1)S(1)}, bf16[96,768]{1,0:T(8,128)(2,1)}, u32[]{:S(2)}, u32[]{:S(2)}) collective-permute-start(bf16[96,768]{1,0:T(8,128)(2,1)S(1)} %get-tuple-element.23), channel_id=1, source_target_pairs={{120,24},{248,152},{376,280},{128,224},{256,352},{384,480},{121,25... | collective-permute-start | bytes 442376 | tf_op jit(solution)/shard_map/ppermute | solution.py:248
  38.9 8.6 %copy-start.3 = (s32[128]{0:T(128)S(1)}, s32[128]{0:T(128)}, u32[]{:S(2)}) copy-start(s32[128]{0:T(128)} %args_1_.4) | copy-start | bytes 1540
  38.9 17.5 %collective-permute-start.4 = (bf16[64,768]{1,0:T(8,128)(2,1)S(1)}, bf16[64,768]{1,0:T(8,128)(2,1)S(1)}, u32[]{:S(2)}, u32[]{:S(2)}) collective-permute-start(bf16[64,768]{1,0:T(8,128)(2,1)S(1)} %slice.9), channel_id=1, source_target_pairs={{120,128},{248,256},{376,384},{128,120},{256,248},{384,376},{121,1... | collective-permute-start | bytes 294920 | tf_op jit(solution)/shard_map/ppermute | solution.py:248
  44.8 14.0 %collective-permute-start.6 = (bf16[96,768]{1,0:T(8,128)(2,1)S(1)}, bf16[96,768]{1,0:T(8,128)(2,1)S(1)}, u32[]{:S(2)}, u32[]{:S(2)}) collective-permute-start(bf16[96,768]{1,0:T(8,128)(2,1)S(1)} %collective-permute-done.5), channel_id=1, source_target_pairs={{96,128},{224,256},{352,384},{152,120},{280,248},{408,376},{97,129... | collective-permute-start | bytes 442376 | tf_op jit(solution)/shard_map/ppermute | solution.py:248
  46.1 14.2 %collective-permute-start.8 = (bf16[96,768]{1,0:T(8,128)(2,1)}, bf16[96,768]{1,0:T(8,128)(2,1)S(1)}, u32[]{:S(2)}, u32[]{:S(2)}) collective-permute-start(bf16[96,768]{1,0:T(8,128)(2,1)} %collective-permute-done.7), channel_id=1, source_target_pairs={{24,128},{152,256},{280,384},{224,120},{352,248},{480,376},{25,129... | collective-permute-start | bytes 442376 | tf_op jit(solution)/shard_map/ppermute | solution.py:248
  51.7 45.4 %collective-permute-start.2 = (bf16[272,768]{1,0:T(8,128)(2,1)S(1)}, bf16[272,768]{1,0:T(8,128)(2,1)S(1)}, u32[]{:S(2)}, u32[]{:S(2)}) collective-permute-start(bf16[272,768]{1,0:T(8,128)(2,1)S(1)} %get-tuple-element.18), channel_id=1, source_target_pairs={{0,8},{8,16},{16,24},{24,32},{32,40},{40,48},{48,56},{56,64},{64,7... | collective-permute-start | bytes 1253384 | tf_op jit(solution)/shard_map/ppermute | solution.py:248
  55.1 41.9 %collective-permute-start.3 = (bf16[272,768]{1,0:T(8,128)(2,1)S(1)}, bf16[272,768]{1,0:T(8,128)(2,1)S(1)}, u32[]{:S(2)}, u32[]{:S(2)}) collective-permute-start(bf16[272,768]{1,0:T(8,128)(2,1)S(1)} %get-tuple-element.19), channel_id=1, source_target_pairs={{8,0},{16,8},{24,16},{32,24},{40,32},{48,40},{56,48},{64,56},{72,6... | collective-permute-start | bytes 1253384 | tf_op jit(solution)/shard_map/ppermute | solution.py:248
  64.6 14.3 %collective-permute-start.10 = (bf16[96,768]{1,0:T(8,128)(2,1)S(1)}, bf16[96,768]{1,0:T(8,128)(2,1)S(1)}, u32[]{:S(2)}, u32[]{:S(2)}) collective-permute-start(bf16[96,768]{1,0:T(8,128)(2,1)S(1)} %get-tuple-element.21), channel_id=1, source_target_pairs={{120,96},{248,224},{376,352},{128,152},{256,280},{384,408},{121,97... | collective-permute-start | bytes 442376 | tf_op jit(solution)/shard_map/ppermute | solution.py:248
  71.7 8.5 %collective-permute-start.12 = (bf16[96,768]{1,0:T(8,128)(2,1)S(1)}, bf16[96,768]{1,0:T(8,128)(2,1)S(1)}, u32[]{:S(2)}, u32[]{:S(2)}) collective-permute-start(bf16[96,768]{1,0:T(8,128)(2,1)S(1)} %get-tuple-element.22), channel_id=1, source_target_pairs={{120,24},{248,152},{376,280},{128,224},{256,352},{384,480},{121,25... | collective-permute-start | bytes 442376 | tf_op jit(solution)/shard_map/ppermute | solution.py:248
  78.9 18.2 %collective-permute-start.11 = (bf16[96,768]{1,0:T(8,128)(2,1)S(1)}, bf16[96,768]{1,0:T(8,128)(2,1)S(1)}, u32[]{:S(2)}, u32[]{:S(2)}) collective-permute-start(bf16[96,768]{1,0:T(8,128)(2,1)S(1)} %collective-permute-done.10), channel_id=1, source_target_pairs={{96,128},{224,256},{352,384},{152,120},{280,248},{408,376},{97,129... | collective-permute-start | bytes 442376 | tf_op jit(solution)/shard_map/ppermute | solution.py:248
  80.2 16.9 %collective-permute-start.13 = (bf16[96,768]{1,0:T(8,128)(2,1)S(1)}, bf16[96,768]{1,0:T(8,128)(2,1)S(1)}, u32[]{:S(2)}, u32[]{:S(2)}) collective-permute-start(bf16[96,768]{1,0:T(8,128)(2,1)S(1)} %collective-permute-done.12), channel_id=1, source_target_pairs={{24,128},{152,256},{280,384},{224,120},{352,248},{480,376},{25,129... | collective-permute-start | bytes 442376 | tf_op jit(solution)/shard_map/ppermute | solution.py:248
  81.5 15.6 %copy-start.2 = (f32[6144]{0:T(1024)S(1)}, f32[6144]{0:T(1024)}, u32[]{:S(2)}) copy-start(f32[6144]{0:T(1024)} %param.15) | copy-start | bytes 73732
  81.5 15.6 %collective-permute-start.9 = (bf16[80,768]{1,0:T(8,128)(2,1)S(1)}, bf16[80,768]{1,0:T(8,128)(2,1)S(1)}, u32[]{:S(2)}, u32[]{:S(2)}) collective-permute-start(bf16[80,768]{1,0:T(8,128)(2,1)S(1)} %get-tuple-element.20), channel_id=1, source_target_pairs={{120,128},{248,256},{376,384},{128,120},{256,248},{384,376},{121,1... | collective-permute-start | bytes 368648 | tf_op jit(solution)/shard_map/ppermute | solution.py:248

commit v2 on v1

--- a/solution.py
+++ b/solution.py
@@ -16,7 +16,8 @@
 LIMIT = 16 << 20
 PLANE = 16
 SIDE = 4
-DETOUR = 96
+Q_DETOUR = 80
+O_DETOUR = 48
 LOG2E = math.log2(math.e)
 NT = (((1,), (1,)), ((), ()))
 
@@ -34,7 +35,7 @@
     used = reached_ref[row]
     times = jnp.int32(0)
     for slot in range(REACH):
-        hit = jnp.logical_and(slot < used, pattern_ref[row, slot] == cached_id)
+        hit = jnp.logical_and(slot < used, pattern_ref[REACH * row + slot] == cached_id)
         times = times + jnp.where(hit, 1, 0)
     bias = jnp.where(times == 1, 0.0, NEGATIVE)
     bias = jnp.where(times == 2, 1.0, bias)
@@ -44,7 +45,7 @@
 
 def fill_bias(bias_ref, pattern_ref, reached_ref, rel_tiles, own_tiles, cached_tiles):
     ctx = lax.axis_index("ctx")
-    tile_count = pattern_ref.shape[0]
+    tile_count = reached_ref.shape[0]
     for row, rel in enumerate(rel_tiles):
         for t in range(own_tiles):
             near = jnp.where(jnp.abs(rel - t) <= 2, 0.0, NEGATIVE)
@@ -247,13 +248,15 @@
     def shift(x, pairs):
         return lax.ppermute(x, "ctx", pairs)
 
+    pattern = pattern.reshape(pattern.size)
+
     def blocks(x):
         return jnp.transpose(x.reshape(part, split, width), (1, 0, 2))
 
     q = lax.all_to_all(blocks(queries), "head", split_axis=0, concat_axis=0, tiled=True).reshape(rows, width)
     kv = jnp.stack([blocks(keys), blocks(values)], axis=1)
     q, kv = lax.optimization_barrier((q, kv))
-    cuts = (rows - 2 * DETOUR, rows - DETOUR)
+    cuts = (rows - 2 * Q_DETOUR, rows - Q_DETOUR)
     jumped = jump([q[: cuts[0]], q[cuts[0] : cuts[1]], q[cuts[1] :]])
     from_below = shift(q, up)
     from_above = shift(q, down)
@@ -279,7 +282,7 @@
     got_low = shift(to_above, up)
     jumped = pl.pallas_call(
         jump_kernel,
-        out_shape=shapes(partial - 2 * DETOUR, DETOUR, DETOUR),
+        out_shape=shapes(partial - 2 * O_DETOUR, O_DETOUR, O_DETOUR),
         in_specs=[smem(), smem()] + [vmem()] * 6,
         out_specs=(vmem(),) * 3,
         scratch_shapes=[pltpu.VMEM((partial, width), jnp.bfloat16), bias],

time: 125 us -> 122 us (0.976)
  the two profiles are of different devices: /device:TPU:128 before, /device:TPU:30 now
where the time goes in v2:
time: 122 us; the launch traced here: 121 us
  starting transfers between devices  48.8 us (40%)
  waiting for transfers between devices  42.2 us (35%)
  blocking collectives  14.9 us (12%)
  Pallas kernels  10.7 us (9%)
  local copies, waits for them, and re-layouts  3.56 us (3%)
    ppermute x14, starting transfers between devices, shift(): return lax.ppermute(x, 'ctx', pairs)  39.1 us
    ppermute x14, waiting for transfers between devices, shift(): return lax.ppermute(x, 'ctx', pairs)  30.8 us
    all_to_all x1, blocking collectives, local(): lax.all_to_all(out.reshape(split, part, width), 'head', split_axis=0, con...  14.9 us
    all_to_all x1, waiting for transfers between devices, local(): lax.all_to_all(blocks(queries), 'head', split_axis=0, concat_axis=0, tile...  11.4 us
    all_to_all x1, starting transfers between devices, local(): lax.all_to_all(blocks(queries), 'head', split_axis=0, concat_axis=0, tile...  6.03 us
    all_to_all x1, starting transfers between devices, local(): kv = lax.all_to_all(kv, 'head', split_axis=0, concat_axis=0, tiled=True)  3.68 us
    pallas_call x1, Pallas kernels, local(): pl.pallas_call(far_kernel, out_shape=shapes(partial, partial), in_specs=[...  3.59 us
    pallas_call x1, Pallas kernels, local(): pl.pallas_call(jump_kernel, out_shape=shapes(partial - 2 * O_DETOUR, O_DE...  3.2 us
  transfers between devices with their start and end apart: 16, of which 8 were waited for; matrix products, arithmetic and copies ran while one was open for 2% of the time, Pallas kernels for 8%

profile of v2, /device:TPU:30, one launch (start us, length us, event | category | flops | bytes accessed | tf_op | source)
XLA Modules:
  0.0 121.4 jit_solution(16271029952324688589)
XLA Ops:
  0.0 1.8 %copy.23 = bf16[4,8,8,768]{3,2,0,1:T(8,128)(2,1)} copy(bf16[4,8,8,768]{3,2,1,0:T(8,128)(2,1)} %bitcast.35) | data formatting | bytes 786432 | tf_op jit(solution)/shard_map/reshape | solution.py:254
  1.8 0.0 copy-start.4
  1.8 0.0 copy-start.5
  1.8 6.0 %all-to-all-start = ((bf16[8,32,768]{2,1,0:T(8,128)(2,1)}), bf16[8,32,768]{2,1,0:T(8,128)(2,1)S(1)}, u32[]{:S(2)}, u32[]{:S(2)}) async-start(bf16[8,32,768]{2,1,0:T(8,128)(2,1)} %bitcast.26), calls=%async_computation | async-start | bytes 786432 | tf_op jit(solution)/shard_map/all_to_all | solution.py:256
  7.8 0.0 copy-done.4
  7.8 0.0 copy-done.5
  7.8 0.1 bitcast_bitcast_fusion
  7.9 1.0 pad_maximum_fusion
  8.9 11.4 %all-to-all-done = bf16[8,32,768]{2,1,0:T(8,128)(2,1)S(1)} async-done(((bf16[8,32,768]{2,1,0:T(8,128)(2,1)}), bf16[8,32,768]{2,1,0:T(8,128)(2,1)S(1)}, u32[]{:S(2)}, u32[]{:S(2)}) %all-to-all-start) | async-done | bytes 393248 | tf_op jit(solution)/shard_map/all_to_all | solution.py:256
  20.3 0.0 copy-start.6
  20.3 0.0 copy-start.1
  20.3 3.7 %all-to-all-start.1 = ((bf16[8,2,32,768]{3,2,1,0:T(8,128)(2,1)}), bf16[8,2,32,768]{3,2,1,0:T(8,128)(2,1)S(1)}, u32[]{:S(2)}, u32[]{:S(2)}) async-start(bf16[8,2,32,768]{3,2,1,0:T(8,128)(2,1)} %pad_maximum_fusion), calls=%async_computation.1 | async-start | bytes 1572864 | tf_op jit(solution)/shard_map/all_to_all | solution.py:263
  24.0 0.0 copy-start
  24.0 1.4 %collective-permute-start = (bf16[256,768]{1,0:T(8,128)(2,1)S(1)}, bf16[256,768]{1,0:T(8,128)(2,1)S(1)}, u32[]{:S(2)}, u32[]{:S(2)}) collective-permute-start(bf16[256,768]{1,0:T(8,128)(2,1)S(1)} %bitcast.27), channel_id=1, source_target_pairs={{0,8},{8,16},{16,24},{24,32},{32,40},{40,48},{48,56},{56,64},{64,7... | collective-permute-start | bytes 1179656 | tf_op jit(solution)/shard_map/ppermute | solution.py:249
  25.5 5.3 %collective-permute-start.1 = (bf16[256,768]{1,0:T(8,128)(2,1)S(1)}, bf16[256,768]{1,0:T(8,128)(2,1)}, u32[]{:S(2)}, u32[]{:S(2)}) collective-permute-start(bf16[256,768]{1,0:T(8,128)(2,1)S(1)} %bitcast.28), channel_id=1, source_target_pairs={{8,0},{16,8},{24,16},{32,24},{40,32},{48,40},{56,48},{64,56},{72,6... | collective-permute-start | bytes 1179656 | tf_op jit(solution)/shard_map/ppermute | solution.py:249
  30.8 4.1 %collective-permute-start.5 = (bf16[80,768]{1,0:T(8,128)(2,1)S(1)}, bf16[80,768]{1,0:T(8,128)(2,1)}, u32[]{:S(2)}, u32[]{:S(2)}) collective-permute-start(bf16[80,768]{1,0:T(8,128)(2,1)S(1)} %get-tuple-element.24), channel_id=1, source_target_pairs={{120,96},{248,224},{376,352},{128,152},{256,280},{384,408},{121,97... | collective-permute-start | bytes 368648 | tf_op jit(solution)/shard_map/ppermute | solution.py:249
  34.9 1.9 %collective-permute-start.7 = (bf16[80,768]{1,0:T(8,128)(2,1)S(1)}, bf16[80,768]{1,0:T(8,128)(2,1)}, u32[]{:S(2)}, u32[]{:S(2)}) collective-permute-start(bf16[80,768]{1,0:T(8,128)(2,1)S(1)} %get-tuple-element.23), channel_id=1, source_target_pairs={{120,24},{248,152},{376,280},{128,224},{256,352},{384,480},{121,25... | collective-permute-start | bytes 368648 | tf_op jit(solution)/shard_map/ppermute | solution.py:249
  36.9 0.0 copy-done.6
  36.9 0.1 copy.11
  37.0 0.1 reshape.24.pattern_ref.args_0_
  37.1 0.0 copy-start.3
  37.1 0.7 slice.9
  37.8 10.6 %collective-permute-start.4 = (bf16[96,768]{1,0:T(8,128)(2,1)}, bf16[96,768]{1,0:T(8,128)(2,1)S(1)}, u32[]{:S(2)}, u32[]{:S(2)}) collective-permute-start(bf16[96,768]{1,0:T(8,128)(2,1)} %slice.9), channel_id=1, source_target_pairs={{120,128},{248,256},{376,384},{128,120},{256,248},{384,376},{121,1... | collective-permute-start | bytes 442376 | tf_op jit(solution)/shard_map/ppermute | solution.py:249
  48.3 0.0 collective-permute-done.5
  48.4 1.3 %collective-permute-start.6 = (bf16[80,768]{1,0:T(8,128)(2,1)}, bf16[80,768]{1,0:T(8,128)(2,1)S(1)}, u32[]{:S(2)}, u32[]{:S(2)}) collective-permute-start(bf16[80,768]{1,0:T(8,128)(2,1)} %collective-permute-done.5), channel_id=1, source_target_pairs={{96,128},{224,256},{352,384},{152,120},{280,248},{408,376},{97,129... | collective-permute-start | bytes 368648 | tf_op jit(solution)/shard_map/ppermute | solution.py:249
  49.7 0.0 collective-permute-done.7
  49.7 1.3 %collective-permute-start.8 = (bf16[80,768]{1,0:T(8,128)(2,1)}, bf16[80,768]{1,0:T(8,128)(2,1)S(1)}, u32[]{:S(2)}, u32[]{:S(2)}) collective-permute-start(bf16[80,768]{1,0:T(8,128)(2,1)} %collective-permute-done.7), channel_id=1, source_target_pairs={{24,128},{152,256},{280,384},{224,120},{352,248},{480,376},{25,129... | collective-permute-start | bytes 368648 | tf_op jit(solution)/shard_map/ppermute | solution.py:249
  51.0 0.0 collective-permute-done.below_ref
  51.0 0.0 collective-permute-done.1.above_ref
  51.0 0.0 all-to-all-done.1.kv_ref.args_5_
  51.0 0.0 copy-done.1
  51.0 0.0 copy-done
  51.0 0.0 copy-done.3
  51.0 3.6 %far.1 = (bf16[272,768]{1,0:T(8,128)(2,1)S(1)}, bf16[272,768]{1,0:T(8,128)(2,1)S(1)}) custom-call(s32[512]{0:T(512)S(1)} %reshape.24.pattern_ref.args_0_, s32[128]{0:T(128)S(1)} %copy-done.3, bf16[256,768]{1,0:T(8,128)(2,1)S(1)} %collective-permute-done.below_ref, bf16[256,768]{1,0:T(8,128)(2,1)} %collective-permute-done.1.above_ref, ...), custom_call_target="tpu_custom_call" | custom-call | flops 1207959552 | bytes 2359296 | tf_op jit(solution)/shard_map/far/pallas_call | solution.py:271
  54.6 1.3 %collective-permute-start.2 = (bf16[272,768]{1,0:T(8,128)(2,1)S(1)}, bf16[272,768]{1,0:T(8,128)(2,1)S(1)}, u32[]{:S(2)}, u32[]{:S(2)}) collective-permute-start(bf16[272,768]{1,0:T(8,128)(2,1)S(1)} %get-tuple-element.18), channel_id=1, source_target_pairs={{0,8},{8,16},{16,24},{24,32},{32,40},{40,48},{48,56},{56,64},{64,7... | collective-permute-start | bytes 1253384 | tf_op jit(solution)/shard_map/ppermute | solution.py:249
  55.9 4.6 %collective-permute-start.3 = (bf16[272,768]{1,0:T(8,128)(2,1)S(1)}, bf16[272,768]{1,0:T(8,128)(2,1)S(1)}, u32[]{:S(2)}, u32[]{:S(2)}) collective-permute-start(bf16[272,768]{1,0:T(8,128)(2,1)S(1)} %get-tuple-element.19), channel_id=1, source_target_pairs={{8,0},{16,8},{24,16},{32,24},{40,32},{48,40},{56,48},{64,56},{72,6... | collective-permute-start | bytes 1253384 | tf_op jit(solution)/shard_map/ppermute | solution.py:249
  60.5 1.7 %collective-permute-done.4.args_2_ = bf16[96,768]{1,0:T(8,128)(2,1)S(1)} collective-permute-done((bf16[96,768]{1,0:T(8,128)(2,1)}, bf16[96,768]{1,0:T(8,128)(2,1)S(1)}, u32[]{:S(2)}, u32[]{:S(2)}) %collective-permute-start.4) | collective-permute-done | bytes 147488 | tf_op jit(solution)/shard_map/ppermute | solution.py:249
  62.2 2.8 %collective-permute-done.6.args_3_ = bf16[80,768]{1,0:T(8,128)(2,1)S(1)} collective-permute-done((bf16[80,768]{1,0:T(8,128)(2,1)}, bf16[80,768]{1,0:T(8,128)(2,1)S(1)}, u32[]{:S(2)}, u32[]{:S(2)}) %collective-permute-start.6) | collective-permute-done | bytes 122912 | tf_op jit(solution)/shard_map/ppermute | solution.py:249
  65.0 1.3 %collective-permute-done.8.args_4_ = bf16[80,768]{1,0:T(8,128)(2,1)S(1)} collective-permute-done((bf16[80,768]{1,0:T(8,128)(2,1)}, bf16[80,768]{1,0:T(8,128)(2,1)S(1)}, u32[]{:S(2)}, u32[]{:S(2)}) %collective-permute-start.8) | collective-permute-done | bytes 122912 | tf_op jit(solution)/shard_map/ppermute | solution.py:249
  66.3 3.2 %jump.1 = (bf16[176,768]{1,0:T(8,128)(2,1)S(1)}, bf16[48,768]{1,0:T(8,128)(2,1)S(1)}, bf16[48,768]{1,0:T(8,128)(2,1)S(1)}) custom-call(s32[512]{0:T(512)S(1)} %reshape.24.pattern_ref.args_0_, s32[128]{0:T(128)S(1)} %copy-done.3, bf16[96,768]{1,0:T(8,128)(2,1)S(1)} %collective-permute-done.4.args_2_, bf16[80,768]{1,0:T(8,128)(2,1)S(1)} %collective-permute-done.6.args_3_, ...), custom_call_target="tpu_custom_call" | custom-call | flops 603979776 | bytes 2359296 | tf_op jit(solution)/shard_map/jump/pallas_call | solution.py:283
  69.5 1.9 %collective-permute-start.9 = (bf16[176,768]{1,0:T(8,128)(2,1)S(1)}, bf16[176,768]{1,0:T(8,128)(2,1)S(1)}, u32[]{:S(2)}, u32[]{:S(2)}) collective-permute-start(bf16[176,768]{1,0:T(8,128)(2,1)S(1)} %get-tuple-element.20), channel_id=1, source_target_pairs={{120,128},{248,256},{376,384},{128,120},{256,248},{384,376},{121,1... | collective-permute-start | bytes 811016 | tf_op jit(solution)/shard_map/ppermute | solution.py:249
  71.5 1.3 %collective-permute-start.10 = (bf16[48,768]{1,0:T(8,128)(2,1)S(1)}, bf16[48,768]{1,0:T(8,128)(2,1)S(1)}, u32[]{:S(2)}, u32[]{:S(2)}) collective-permute-start(bf16[48,768]{1,0:T(8,128)(2,1)S(1)} %get-tuple-element.21), channel_id=1, source_target_pairs={{120,96},{248,224},{376,352},{128,152},{256,280},{384,408},{121,97... | collective-permute-start | bytes 221192 | tf_op jit(solution)/shard_map/ppermute | solution.py:249
  72.8 0.0 copy-start.2
  72.8 1.3 %collective-permute-start.12 = (bf16[48,768]{1,0:T(8,128)(2,1)S(1)}, bf16[48,768]{1,0:T(8,128)(2,1)S(1)}, u32[]{:S(2)}, u32[]{:S(2)}) collective-permute-start(bf16[48,768]{1,0:T(8,128)(2,1)S(1)} %get-tuple-element.22), channel_id=1, source_target_pairs={{120,24},{248,152},{376,280},{128,224},{256,352},{384,480},{121,25... | collective-permute-start | bytes 221192 | tf_op jit(solution)/shard_map/ppermute | solution.py:249
  74.1 0.6 collective-permute-done.10
  74.7 1.3 %collective-permute-start.11 = (bf16[48,768]{1,0:T(8,128)(2,1)S(1)}, bf16[48,768]{1,0:T(8,128)(2,1)S(1)}, u32[]{:S(2)}, u32[]{:S(2)}) collective-permute-start(bf16[48,768]{1,0:T(8,128)(2,1)S(1)} %collective-permute-done.10), channel_id=1, source_target_pairs={{96,128},{224,256},{352,384},{152,120},{280,248},{408,376},{97,129... | collective-permute-start | bytes 221192 | tf_op jit(solution)/shard_map/ppermute | solution.py:249
  76.0 0.0 collective-permute-done.12
  76.1 1.5 %collective-permute-start.13 = (bf16[48,768]{1,0:T(8,128)(2,1)S(1)}, bf16[48,768]{1,0:T(8,128)(2,1)S(1)}, u32[]{:S(2)}, u32[]{:S(2)}) collective-permute-start(bf16[48,768]{1,0:T(8,128)(2,1)S(1)} %collective-permute-done.12), channel_id=1, source_target_pairs={{24,128},{152,256},{280,384},{224,120},{352,248},{480,376},{25,129... | collective-permute-start | bytes 221192 | tf_op jit(solution)/shard_map/ppermute | solution.py:249
  77.5 3.1 %own.1 = (f32[256,768]{1,0:T(8,128)S(1)}, f32[256,128]{1,0:T(8,128)S(1)}) custom-call(s32[512]{0:T(512)S(1)} %reshape.24.pattern_ref.args_0_, s32[128]{0:T(128)S(1)} %copy-done.3, bf16[256,768]{1,0:T(8,128)(2,1)S(1)} %bitcast.31, bf16[8,2,32,768]{3,2,1,0:T(8,128)(2,1)S(1)} %all-to-all-done.1.kv_ref.args_5_, bf16[512,768]{1,0:T(8,128)(2,1)S(1)} %copy-done, ...), custom_call_target="tpu_custom_call" | custom-call | flops 603979776 | bytes 2359296 | tf_op jit(solution)/shard_map/own/pallas_call | solution.py:294
  80.6 8.9 %collective-permute-done.11.part1_ref = bf16[48,768]{1,0:T(8,128)(2,1)S(1)} collective-permute-done((bf16[48,768]{1,0:T(8,128)(2,1)S(1)}, bf16[48,768]{1,0:T(8,128)(2,1)S(1)}, u32[]{:S(2)}, u32[]{:S(2)}) %collective-permute-start.11) | collective-permute-done | bytes 73760 | tf_op jit(solution)/shard_map/ppermute | solution.py:249
  89.5 11.2 %collective-permute-done.13.part2_ref = bf16[48,768]{1,0:T(8,128)(2,1)S(1)} collective-permute-done((bf16[48,768]{1,0:T(8,128)(2,1)S(1)}, bf16[48,768]{1,0:T(8,128)(2,1)S(1)}, u32[]{:S(2)}, u32[]{:S(2)}) %collective-permute-start.13) | collective-permute-done | bytes 73760 | tf_op jit(solution)/shard_map/ppermute | solution.py:249
  100.8 4.1 %collective-permute-done.9.part0_ref = bf16[176,768]{1,0:T(8,128)(2,1)S(1)} collective-permute-done((bf16[176,768]{1,0:T(8,128)(2,1)S(1)}, bf16[176,768]{1,0:T(8,128)(2,1)S(1)}, u32[]{:S(2)}, u32[]{:S(2)}) %collective-permute-start.9) | collective-permute-done | bytes 270368 | tf_op jit(solution)/shard_map/ppermute | solution.py:249
  104.9 0.0 collective-permute-done.2.low_ref
  104.9 0.0 collective-permute-done.3.high_ref
  104.9 0.0 copy-done.2
  104.9 0.8 mix.1
  105.7 14.9 %all_to_all.15 = bf16[8,32,768]{2,1,0:T(8,128)(2,1)S(1)} all-to-all(bf16[8,32,768]{2,1,0:T(8,128)(2,1)S(1)} %bitcast.32), channel_id=1, replica_groups=mesh['ctx'=64,'head'=8] {'head'}, dimensions={0} | all-to-all | bytes 786432 | tf_op jit(solution)/shard_map/all_to_all | solution.py:315
  120.6 0.8 copy.19
  (1 shorter events, 0.0 us)
Async XLA Ops:
  1.8 6.0 %copy-start.4 = (bf16[32,6144]{1,0:T(8,128)(2,1)S(1)}, bf16[32,6144]{1,0:T(8,128)(2,1)}, u32[]{:S(2)}) copy-start(bf16[32,6144]{1,0:T(8,128)(2,1)} %param.10) | copy-start | bytes 1179652
  1.8 6.0 %copy-start.5 = (bf16[32,6144]{1,0:T(8,128)(2,1)S(1)}, bf16[32,6144]{1,0:T(8,128)(2,1)}, u32[]{:S(2)}) copy-start(bf16[32,6144]{1,0:T(8,128)(2,1)} %param.9) | copy-start | bytes 1179652
  1.8 18.6 %all-to-all-start = ((bf16[8,32,768]{2,1,0:T(8,128)(2,1)}), bf16[8,32,768]{2,1,0:T(8,128)(2,1)S(1)}, u32[]{:S(2)}, u32[]{:S(2)}) async-start(bf16[8,32,768]{2,1,0:T(8,128)(2,1)} %bitcast.26), calls=%async_computation | async-start | bytes 786432 | tf_op jit(solution)/shard_map/all_to_all | solution.py:256
  20.3 16.5 %copy-start.6 = (s32[128,4]{0,1:T(4,128)S(1)}, s32[128,4]{0,1:T(4,128)}, u32[]{:S(2)}) copy-start(s32[128,4]{0,1:T(4,128)} %param.13) | copy-start | bytes 6148
  20.3 30.7 %copy-start.1 = (bf16[512,768]{1,0:T(8,128)(2,1)S(1)}, bf16[512,768]{1,0:T(8,128)(2,1)}, u32[]{:S(2)}) copy-start(bf16[512,768]{1,0:T(8,128)(2,1)} %args_7_.4) | copy-start | bytes 2359300
  20.3 30.7 %all-to-all-start.1 = ((bf16[8,2,32,768]{3,2,1,0:T(8,128)(2,1)}), bf16[8,2,32,768]{3,2,1,0:T(8,128)(2,1)S(1)}, u32[]{:S(2)}, u32[]{:S(2)}) async-start(bf16[8,2,32,768]{3,2,1,0:T(8,128)(2,1)} %pad_maximum_fusion), calls=%async_computation.1 | async-start | bytes 1572864 | tf_op jit(solution)/shard_map/all_to_all | solution.py:263
  24.0 27.0 %copy-start = (bf16[512,768]{1,0:T(8,128)(2,1)S(1)}, bf16[512,768]{1,0:T(8,128)(2,1)}, u32[]{:S(2)}) copy-start(bf16[512,768]{1,0:T(8,128)(2,1)} %args_6_.4) | copy-start | bytes 2359300
  24.0 26.9 %collective-permute-start = (bf16[256,768]{1,0:T(8,128)(2,1)S(1)}, bf16[256,768]{1,0:T(8,128)(2,1)S(1)}, u32[]{:S(2)}, u32[]{:S(2)}) collective-permute-start(bf16[256,768]{1,0:T(8,128)(2,1)S(1)} %bitcast.27), channel_id=1, source_target_pairs={{0,8},{8,16},{16,24},{24,32},{32,40},{40,48},{48,56},{56,64},{64,7... | collective-permute-start | bytes 1179656 | tf_op jit(solution)/shard_map/ppermute | solution.py:249
  25.5 25.5 %collective-permute-start.1 = (bf16[256,768]{1,0:T(8,128)(2,1)S(1)}, bf16[256,768]{1,0:T(8,128)(2,1)}, u32[]{:S(2)}, u32[]{:S(2)}) collective-permute-start(bf16[256,768]{1,0:T(8,128)(2,1)S(1)} %bitcast.28), channel_id=1, source_target_pairs={{8,0},{16,8},{24,16},{32,24},{40,32},{48,40},{56,48},{64,56},{72,6... | collective-permute-start | bytes 1179656 | tf_op jit(solution)/shard_map/ppermute | solution.py:249
  30.8 17.6 %collective-permute-start.5 = (bf16[80,768]{1,0:T(8,128)(2,1)S(1)}, bf16[80,768]{1,0:T(8,128)(2,1)}, u32[]{:S(2)}, u32[]{:S(2)}) collective-permute-start(bf16[80,768]{1,0:T(8,128)(2,1)S(1)} %get-tuple-element.24), channel_id=1, source_target_pairs={{120,96},{248,224},{376,352},{128,152},{256,280},{384,408},{121,97... | collective-permute-start | bytes 368648 | tf_op jit(solution)/shard_map/ppermute | solution.py:249
  34.9 14.7 %collective-permute-start.7 = (bf16[80,768]{1,0:T(8,128)(2,1)S(1)}, bf16[80,768]{1,0:T(8,128)(2,1)}, u32[]{:S(2)}, u32[]{:S(2)}) collective-permute-start(bf16[80,768]{1,0:T(8,128)(2,1)S(1)} %get-tuple-element.23), channel_id=1, source_target_pairs={{120,24},{248,152},{376,280},{128,224},{256,352},{384,480},{121,25... | collective-permute-start | bytes 368648 | tf_op jit(solution)/shard_map/ppermute | solution.py:249
  37.1 13.9 %copy-start.3 = (s32[128]{0:T(128)S(1)}, s32[128]{0:T(128)}, u32[]{:S(2)}) copy-start(s32[128]{0:T(128)} %args_1_.4) | copy-start | bytes 1540
  37.8 24.4 %collective-permute-start.4 = (bf16[96,768]{1,0:T(8,128)(2,1)}, bf16[96,768]{1,0:T(8,128)(2,1)S(1)}, u32[]{:S(2)}, u32[]{:S(2)}) collective-permute-start(bf16[96,768]{1,0:T(8,128)(2,1)} %slice.9), channel_id=1, source_target_pairs={{120,128},{248,256},{376,384},{128,120},{256,248},{384,376},{121,1... | collective-permute-start | bytes 442376 | tf_op jit(solution)/shard_map/ppermute | solution.py:249
  48.4 16.7 %collective-permute-start.6 = (bf16[80,768]{1,0:T(8,128)(2,1)}, bf16[80,768]{1,0:T(8,128)(2,1)S(1)}, u32[]{:S(2)}, u32[]{:S(2)}) collective-permute-start(bf16[80,768]{1,0:T(8,128)(2,1)} %collective-permute-done.5), channel_id=1, source_target_pairs={{96,128},{224,256},{352,384},{152,120},{280,248},{408,376},{97,129... | collective-permute-start | bytes 368648 | tf_op jit(solution)/shard_map/ppermute | solution.py:249
  49.7 16.7 %collective-permute-start.8 = (bf16[80,768]{1,0:T(8,128)(2,1)}, bf16[80,768]{1,0:T(8,128)(2,1)S(1)}, u32[]{:S(2)}, u32[]{:S(2)}) collective-permute-start(bf16[80,768]{1,0:T(8,128)(2,1)} %collective-permute-done.7), channel_id=1, source_target_pairs={{24,128},{152,256},{280,384},{224,120},{352,248},{480,376},{25,129... | collective-permute-start | bytes 368648 | tf_op jit(solution)/shard_map/ppermute | solution.py:249
  54.6 50.3 %collective-permute-start.2 = (bf16[272,768]{1,0:T(8,128)(2,1)S(1)}, bf16[272,768]{1,0:T(8,128)(2,1)S(1)}, u32[]{:S(2)}, u32[]{:S(2)}) collective-permute-start(bf16[272,768]{1,0:T(8,128)(2,1)S(1)} %get-tuple-element.18), channel_id=1, source_target_pairs={{0,8},{8,16},{16,24},{24,32},{32,40},{40,48},{48,56},{56,64},{64,7... | collective-permute-start | bytes 1253384 | tf_op jit(solution)/shard_map/ppermute | solution.py:249
  55.9 49.0 %collective-permute-start.3 = (bf16[272,768]{1,0:T(8,128)(2,1)S(1)}, bf16[272,768]{1,0:T(8,128)(2,1)S(1)}, u32[]{:S(2)}, u32[]{:S(2)}) collective-permute-start(bf16[272,768]{1,0:T(8,128)(2,1)S(1)} %get-tuple-element.19), channel_id=1, source_target_pairs={{8,0},{16,8},{24,16},{32,24},{40,32},{48,40},{56,48},{64,56},{72,6... | collective-permute-start | bytes 1253384 | tf_op jit(solution)/shard_map/ppermute | solution.py:249
  69.5 35.3 %collective-permute-start.9 = (bf16[176,768]{1,0:T(8,128)(2,1)S(1)}, bf16[176,768]{1,0:T(8,128)(2,1)S(1)}, u32[]{:S(2)}, u32[]{:S(2)}) collective-permute-start(bf16[176,768]{1,0:T(8,128)(2,1)S(1)} %get-tuple-element.20), channel_id=1, source_target_pairs={{120,128},{248,256},{376,384},{128,120},{256,248},{384,376},{121,1... | collective-permute-start | bytes 811016 | tf_op jit(solution)/shard_map/ppermute | solution.py:249
  71.5 3.3 %collective-permute-start.10 = (bf16[48,768]{1,0:T(8,128)(2,1)S(1)}, bf16[48,768]{1,0:T(8,128)(2,1)S(1)}, u32[]{:S(2)}, u32[]{:S(2)}) collective-permute-start(bf16[48,768]{1,0:T(8,128)(2,1)S(1)} %get-tuple-element.21), channel_id=1, source_target_pairs={{120,96},{248,224},{376,352},{128,152},{256,280},{384,408},{121,97... | collective-permute-start | bytes 221192 | tf_op jit(solution)/shard_map/ppermute | solution.py:249
  72.8 32.1 %copy-start.2 = (f32[6144]{0:T(1024)S(1)}, f32[6144]{0:T(1024)}, u32[]{:S(2)}) copy-start(f32[6144]{0:T(1024)} %param.15) | copy-start | bytes 73732
  72.8 3.3 %collective-permute-start.12 = (bf16[48,768]{1,0:T(8,128)(2,1)S(1)}, bf16[48,768]{1,0:T(8,128)(2,1)S(1)}, u32[]{:S(2)}, u32[]{:S(2)}) collective-permute-start(bf16[48,768]{1,0:T(8,128)(2,1)S(1)} %get-tuple-element.22), channel_id=1, source_target_pairs={{120,24},{248,152},{376,280},{128,224},{256,352},{384,480},{121,25... | collective-permute-start | bytes 221192 | tf_op jit(solution)/shard_map/ppermute | solution.py:249
  74.7 14.8 %collective-permute-start.11 = (bf16[48,768]{1,0:T(8,128)(2,1)S(1)}, bf16[48,768]{1,0:T(8,128)(2,1)S(1)}, u32[]{:S(2)}, u32[]{:S(2)}) collective-permute-start(bf16[48,768]{1,0:T(8,128)(2,1)S(1)} %collective-permute-done.10), channel_id=1, source_target_pairs={{96,128},{224,256},{352,384},{152,120},{280,248},{408,376},{97,129... | collective-permute-start | bytes 221192 | tf_op jit(solution)/shard_map/ppermute | solution.py:249
  76.1 24.7 %collective-permute-start.13 = (bf16[48,768]{1,0:T(8,128)(2,1)S(1)}, bf16[48,768]{1,0:T(8,128)(2,1)S(1)}, u32[]{:S(2)}, u32[]{:S(2)}) collective-permute-start(bf16[48,768]{1,0:T(8,128)(2,1)S(1)} %collective-permute-done.12), channel_id=1, source_target_pairs={{24,128},{152,256},{280,384},{224,120},{352,248},{480,376},{25,129... | collective-permute-start | bytes 221192 | tf_op jit(solution)/shard_map/ppermute | solution.py:249
